TPU v7x, 256 devices: a whole 4x4x8 slice. The times are simulated.
256 devices in a mesh: roll: 32 (over y_lo, z, core), trans: 8 (over y_hi, x).
Axes of the slice: x: 4, y: 4 (y_hi: 2, y_lo: 2; y = y_hi * 2 + y_lo), z: 8, core: 2. Of those that a mesh axis runs over, the one named last changes fastest.
Arguments:
- adjoint: float32 [4, 2, 32, 256, 1024], P(None, None, None, 'roll', 'trans'), may hold values from -6 to 6
- source: float32 [4, 2, 32, 256, 1024], P(None, None, None, 'roll', 'trans'), may hold values from -6 to 6
- pressure: float32 [2, 256, 1024], P(None, 'roll', 'trans'), may hold values from -4 to 4
- film: float32 [256, 1024], P('roll', 'trans'), may hold values from 0.6 to 1.4
- cavity: int32 [2, 256, 1024], P(None, 'roll', 'trans'), may hold values 0 or 1
- temp_index: int32 [2], replicated, may hold values from 0 to 7
Outputs:
- adjoint_out: float32 [4, 2, 32, 256, 1024], P(None, None, None, 'roll', 'trans')
- wall_step: float32 [256, 1024], P('roll', 'trans')
All inputs are finite; a program needn't handle non-finite values. No bound on the sum of `cavity` on one device may be relied on, other than what follows from the above.
Results may differ from a plain program's by a relative error of at most 0.00002.
Values sent between devices are 32-bit elements; how exact they have to be, the bound alone decides.
A program may use at most 64 MiB of HBM per device.

v0:
```python
import jax
import jax.numpy as jnp
from jax import lax
from jax.sharding import PartitionSpec as P

SECTIONS = 2


VISCOSITY_PRESS = 0.3
VISCOSITY_TEMP = 0.5
THETA_STEP = 0.2
SOUND = 0.5
KAPPA = 0.6
HEATING = 0.3
ROLL_SPEED = 1.0
COURANT = 0.8


def extended(array, sides, width):
    for axis, dim in sides:
        size, length = (lax.axis_size(axis), array.shape[dim])
        up = [(i, (i + 1) % size) for i in range(size - 1)]
        down = [(j, i) for i, j in up]
        last = lax.slice_in_dim(array, length - width, length, axis=dim)
        leading = lax.slice_in_dim(array, 0, width, axis=dim)
        before = lax.ppermute(last, axis, up)
        after = lax.ppermute(leading, axis, down)
        array = jnp.concatenate([before, array, after], axis=dim)
    return array


def coefficients(pressure, film, cavity, temp_index):
    implicit_weight = THETA_STEP * temp_index.astype(jnp.float32)
    fluid_viscosity = jnp.exp(
        VISCOSITY_PRESS * pressure - VISCOSITY_TEMP * implicit_weight[:, None, None]
    )
    film_coef = 4.0 * fluid_viscosity / (film * film)
    density = 1.0 - 0.6 * cavity.astype(jnp.float32)
    pseudo_step = COURANT / (32.0 / 3.0 * fluid_viscosity + 4.0 * film_coef + 2.0 * SOUND + 1.0)
    return jnp.stack([fluid_viscosity, film_coef, density, pseudo_step])


def time_section(padded, source, coeffs):
    depth = source.shape[-3]
    width_x = source.shape[-2]
    width_y = source.shape[-1]

    def along_x(offset):
        return padded[..., 2 + offset : 2 + offset + width_x, 2 : 2 + width_y]

    def along_y(offset):
        return padded[..., 2 : 2 + width_x, 2 + offset : 2 + offset + width_y]

    center = along_x(0)
    second_x = (
        -along_x(2) + 16.0 * along_x(1) - 30.0 * center + 16.0 * along_x(-1) - along_x(-2)
    ) / 12.0
    second_y = (
        -along_y(2) + 16.0 * along_y(1) - 30.0 * center + 16.0 * along_y(-1) - along_y(-2)
    ) / 12.0
    first_x = (-along_x(2) + 8.0 * along_x(1) - 8.0 * along_x(-1) + along_x(-2)) / 12.0
    first_y = (-along_y(2) + 8.0 * along_y(1) - 8.0 * along_y(-1) + along_y(-2)) / 12.0
    layered = jnp.pad(center, ((0, 0), (0, 0), (1, 1), (0, 0), (0, 0)))
    second_z = layered[:, :, 2:] - 2.0 * center + layered[:, :, :-2]
    fluid_viscosity = coeffs[0][:, None]
    film_coef = coeffs[1][:, None]
    density = coeffs[2][:, None]
    pseudo_step = coeffs[3][:, None]
    film_height = ((jnp.arange(depth).astype(jnp.float32) + 0.5) / depth)[:, None, None]
    diffused = fluid_viscosity * (second_x + second_y) + film_coef * second_z
    carried = density * ROLL_SPEED * film_height * first_x
    resid_density = 0.5 * diffused[0] + carried[0] + SOUND * (first_x[1] + first_y[2])
    resid_along = diffused[1] + carried[1] + SOUND * first_x[0]
    resid_across = diffused[2] + carried[2] + SOUND * first_y[0]
    resid_energy = KAPPA * diffused[3] + carried[3] + HEATING * fluid_viscosity * center[1]
    residual = jnp.stack([resid_density, resid_along, resid_across, resid_energy])
    return center + pseudo_step * (residual + source)


def wall_terms(padded_mean, momentum, coeffs, film):
    width_x = momentum.shape[-2]
    depth = momentum.shape[-3]
    slope = (
        -padded_mean[:, 4 : 4 + width_x]
        + 8.0 * padded_mean[:, 3 : 3 + width_x]
        - 8.0 * padded_mean[:, 1 : 1 + width_x]
        + padded_mean[:, 0:width_x]
    ) / 12.0
    layered = jnp.pad(momentum, ((0, 0), (1, 1), (0, 0), (0, 0)))
    bending = layered[:, 2:] - 2.0 * momentum + layered[:, :-2]
    curvature = jnp.sum(momentum * bending, axis=1) / depth
    flux = coeffs[2] * ROLL_SPEED * film / 2.0
    return flux * slope - 8.0 * coeffs[0] / (film * film * film) * curvature


def on_device(adjoint, source, pressure, film, cavity, temp_index):
    coeffs = coefficients(pressure, film, cavity, temp_index)
    depth = adjoint.shape[2]
    state = adjoint
    for section_index in range(SECTIONS):
        padded = extended(state, (("roll", 3), ("trans", 4)), 2)
        state = time_section(padded, source, coeffs)
    mean_density = jnp.sum(state[0], axis=1) / depth
    padded_mean = extended(mean_density, (("roll", 1),), 2)
    terms = wall_terms(padded_mean, state[1], coeffs, film)
    wall_grad = jnp.sum(terms, axis=0)
    total = lax.psum(jnp.sum(wall_grad * wall_grad), ("roll", "trans"))
    cell_count = (
        wall_grad.shape[0] * wall_grad.shape[1] * lax.axis_size("roll") * lax.axis_size("trans")
    )
    wall_step = wall_grad / jnp.sqrt(total / cell_count + 1e-06)
    return (state, wall_step)


def solution(mesh):
    placed = (
        P(None, None, None, "roll", "trans"),
        P(None, None, None, "roll", "trans"),
        P(None, "roll", "trans"),
        P("roll", "trans"),
        P(None, "roll", "trans"),
        P(),
    )
    return jax.shard_map(
        on_device,
        mesh=mesh,
        in_specs=placed,
        out_specs=(P(None, None, None, "roll", "trans"), P("roll", "trans")),
        check_vma=False,
    )
```

profile of v0, /device:TPU:1, one launch (start us, length us, event | category | flops | bytes accessed | tf_op | source)
XLA Modules:
  0.0 192.9 jit_solution(15811736756674516837)
XLA Ops:
  0.7 1.5 copy.205
  2.9 4.9 %collective-permute-start.1 = (f32[4,2,32,2,128]{4,2,3,1,0:T(8,128)S(1)}, f32[4,2,32,2,128]{4,2,3,1,0:T(8,128)}, u32[]{:S(2)}, u32[]{:S(2)}) collective-permute-start(f32[4,2,32,2,128]{4,2,3,1,0:T(8,128)S(1)} %get-tuple-element.33), channel_id=1, source_target_pairs={{0,8},{8,16},{16,24},{24,32},{32,40},{40,48},{48,56},{56,64},{64,7... | collective-permute-start | bytes 786440 | tf_op jit(solution)/shard_map/ppermute | solution.py:26
  7.9 2.2 %collective-permute-start = (f32[4,2,32,2,128]{4,2,3,1,0:T(8,128)}, f32[4,2,32,2,128]{4,2,3,1,0:T(8,128)S(1)}, u32[]{:S(2)}, u32[]{:S(2)}) collective-permute-start(f32[4,2,32,2,128]{4,2,3,1,0:T(8,128)} %get-tuple-element.32), channel_id=1, source_target_pairs={{8,0},{16,8},{24,16},{32,24},{40,32},{48,40},{56,48},{64,56},{72,6... | collective-permute-start | bytes 786440 | tf_op jit(solution)/shard_map/ppermute | solution.py:27
  11.4 2.7 %copy.195 = f32[4,2,32,8,128]{2,3,4,1,0:T(8,128)} copy(f32[4,2,32,8,128]{4,3,2,1,0:T(8,128)S(1)} %copy-done.1) | data formatting | bytes 2097152 | tf_op args[0]
  14.9 1.4 copy.194
  16.4 1.3 copy.196
  17.7 3.7 %pad_maximum_fusion = f32[4,2,32,12,128]{2,3,4,1,0:T(8,128)S(1)} fusion(f32[4,2,32,2,128]{2,3,4,1,0:T(2,128)} %copy.196, f32[4,2,32,8,128]{2,3,4,1,0:T(8,128)} %copy.195, f32[4,2,32,2,128]{2,3,4,1,0:T(2,128)S(1)} %copy.194), kind=kLoop, calls=%fused_computation | loop fusion | flops 786432 | bytes 3145728 | tf_op jit(solution)/shard_map/concatenate | solution.py:28
  22.1 1.3 collective-permute-start.2
  23.4 4.6 %collective-permute-start.3 = (f32[4,2,32,12,2]{2,3,4,1,0:T(8,128)S(1)}, f32[4,2,32,12,2]{2,3,4,1,0:T(8,128)}, u32[]{:S(2)}, u32[]{:S(2)}) collective-permute-start(f32[4,2,32,12,2]{2,3,4,1,0:T(8,128)S(1)} %get-tuple-element.16), channel_id=1, source_target_pairs={{0,1},{1,2},{2,3},{3,4},{4,5},{5,6},{6,7},{8,9},{9,10},{10,11},{11... | collective-permute-start | bytes 73736 | tf_op jit(solution)/shard_map/ppermute | solution.py:26
  30.0 1.3 broadcast_multiply_fusion.2
  32.4 6.1 %copy.197 = f32[4,2,32,12,128]{4,2,3,1,0:T(8,128)} copy(f32[4,2,32,12,128]{2,3,4,1,0:T(8,128)} %copy-done) | data formatting | bytes 3145728 | tf_op jit(solution)/shard_map/concatenate | solution.py:28
  38.5 2.7 %copy.198 = f32[4,2,32,12,2]{4,2,3,1,0:T(8,128)} copy(f32[4,2,32,12,2]{2,3,4,1,0:T(8,128)} %collective-permute-done.2) | data formatting | bytes 49152 | tf_op jit(solution)/shard_map/ppermute | solution.py:27
  41.2 2.7 %copy.199 = f32[4,2,32,12,2]{4,2,3,1,0:T(8,128)} copy(f32[4,2,32,12,2]{2,3,4,1,0:T(8,128)} %collective-permute-done.3) | data formatting | bytes 49152 | tf_op jit(solution)/shard_map/ppermute | solution.py:26
  43.9 5.9 %add_multiply_fusion.1 = f32[4,2,32,8,128]{4,2,3,1,0:T(8,128)S(1)} fusion(f32[4,2,32,12,2]{4,2,3,1,0:T(8,128)} %copy.198, f32[4,2,32,12,128]{4,2,3,1,0:T(8,128)} %copy.197, f32[4,2,32,12,2]{4,2,3,1,0:T(8,128)} %copy.199), kind=kLoop, calls=%fused_computation.44 | loop fusion | flops 2883584 | bytes 2670592 | tf_op jit(solution)/shard_map/div | solution.py:62
  49.9 3.5 %fusion.6 = f32[4,2,32,8,128]{4,2,3,1,0:T(8,128)S(1)} fusion(f32[4,2,32,8,128]{4,2,3,1,0:T(8,128)S(1)} %copy.205, f32[4,2,32,10,128]{4,2,3,1,0:T(8,128)S(1)} %copy-done.3, f32[4,2,32,10,128]{4,2,3,1,0:T(8,128)S(1)} %constant_dynamic-update-slice_fusion, f32[2,8,128]{2,1,0:T(8,128)S(1)} %copy-done.18, f32[2,8,128]{2,1,0:T(8,128)S(1)} %copy-done.17, ...), kind=kLoop, calls=%fused_computation.16 | loop fusion | flops 6815744 | bytes 7929856 | tf_op jit(solution)/shard_map/add | solution.py:70
  55.2 1.9 collective-permute-start.4
  57.1 3.9 %collective-permute-start.5 = (f32[4,2,32,2,128]{4,2,3,1,0:T(8,128)S(1)}, f32[4,2,32,2,128]{4,2,3,1,0:T(8,128)S(1)}, u32[]{:S(2)}, u32[]{:S(2)}) collective-permute-start(f32[4,2,32,2,128]{4,2,3,1,0:T(8,128)S(1)} %get-tuple-element.31), channel_id=1, source_target_pairs={{0,8},{8,16},{16,24},{24,32},{32,40},{40,48},{48,56},{56,64},{64,7... | collective-permute-start | bytes 786440 | tf_op jit(solution)/shard_map/ppermute | solution.py:26
  61.0 2.1 %collective-permute-done.4 = f32[4,2,32,2,128]{4,2,3,1,0:T(8,128)S(1)} collective-permute-done((f32[4,2,32,2,128]{4,2,3,1,0:T(8,128)S(1)}, f32[4,2,32,2,128]{4,2,3,1,0:T(8,128)S(1)}, u32[]{:S(2)}, u32[]{:S(2)}) %collective-permute-start.4) | collective-permute-done | bytes 262176 | tf_op jit(solution)/shard_map/ppermute | solution.py:27
  64.4 2.2 %fusion.42 = (f32[4,2,32,12,2]{4,2,3,1,0:T(8,128)}, f32[4,2,32,12,2]{4,2,3,1,0:T(8,128)}) fusion(f32[4,2,32,12,128]{4,2,3,1,0:T(8,128)S(1)} %pad_maximum_fusion.1), kind=kLoop, calls=%fused_computation.124 | loop fusion | bytes 98304 | tf_op jit(solution)/shard_map/slice | solution.py:24
  66.6 2.2 %copy.218 = f32[4,2,32,12,2]{2,3,4,1,0:T(8,128)S(1)} copy(f32[4,2,32,12,2]{4,2,3,1,0:T(8,128)} %get-tuple-element.27) | data formatting | bytes 49152
  68.8 1.3 collective-permute-start.6
  70.1 2.2 %copy.219 = f32[4,2,32,12,2]{2,3,4,1,0:T(8,128)S(1)} copy(f32[4,2,32,12,2]{4,2,3,1,0:T(8,128)} %get-tuple-element.26) | data formatting | bytes 49152
  72.4 4.3 %collective-permute-start.7 = (f32[4,2,32,12,2]{2,3,4,1,0:T(8,128)S(1)}, f32[4,2,32,12,2]{2,3,4,1,0:T(8,128)S(1)}, u32[]{:S(2)}, u32[]{:S(2)}) collective-permute-start(f32[4,2,32,12,2]{2,3,4,1,0:T(8,128)S(1)} %copy.219), channel_id=1, source_target_pairs={{0,1},{1,2},{2,3},{3,4},{4,5},{5,6},{6,7},{8,9},{9,10},{10,11},{11... | collective-permute-start | bytes 73736 | tf_op jit(solution)/shard_map/ppermute | solution.py:26
  76.7 1.3 broadcast_multiply_fusion.3
  78.1 1.8 copy.207
  80.0 1.8 copy.209
  81.8 4.0 %fusion.10 = f32[4,2,32,8,128]{4,2,3,1,0:T(8,128)S(1)} fusion(f32[4,2,32,8,128]{4,2,3,1,0:T(8,128)S(1)} %fusion.12, f32[4,2,32,2,128]{4,2,3,1,0:T(8,128)S(1)} %collective-permute-done.4, f32[4,2,32,2,128]{4,2,3,1,0:T(8,128)S(1)} %collective-permute-done.5, f32[2,8,128]{2,1,0:T(8,128)S(1)} %copy-done.18, f32[2,8,128]{2,1,0:T(8,128)S(1)} %copy-done.17, ...), kind=kLoop, calls=%fused_computation.20 | loop fusion | flops 9961472 | bytes 2686976 | tf_op jit(solution)/shard_map/add | solution.py:70
  85.9 2.0 %add_multiply_fusion = f32[4,2,32,8,128]{4,2,3,1,0:T(8,128)S(1)} fusion(f32[4,2,32,12,2]{4,2,3,1,0:T(8,128)S(1)} %copy-done.5, f32[4,2,32,2,128]{4,2,3,1,0:T(8,128)S(1)} %collective-permute-done.4, f32[4,2,32,8,128]{4,2,3,1,0:T(8,128)S(1)} %fusion.12, f32[4,2,32,2,128]{4,2,3,1,0:T(8,128)S(1)} %collective-permute-done.5, f32[4,2,32,12,2]{4,2,3,1,0:T(8,128)S(1)} %copy-done.6), kind=kLoop, calls=%fused_computation.42 | loop fusion | flops 4980736 | bytes 2670592 | tf_op jit(solution)/shard_map/div | solution.py:62
  89.6 1.9 collective-permute-start.8
  91.5 4.9 %collective-permute-start.9 = (f32[2,2,128]{2,1,0:T(2,128)S(1)}, f32[2,2,128]{2,1,0:T(2,128)S(1)}, u32[]{:S(2)}, u32[]{:S(2)}) collective-permute-start(f32[2,2,128]{2,1,0:T(2,128)S(1)} %get-tuple-element.43), channel_id=1, source_target_pairs={{0,8},{8,16},{16,24},{24,32},{32,40},{40,48},{48,56},{56,64},{64,7... | collective-permute-start | bytes 6152 | tf_op jit(solution)/shard_map/ppermute | solution.py:26
  97.9 1.6 copy.215
  99.5 92.1 %psum.7 = f32[]{:T(128)} all-reduce(f32[]{:T(128)} %multiply_reduce_fusion), channel_id=1, replica_groups=mesh['roll'=32,'trans'=8] {'roll','trans'}, use_global_device_ids=true, to_apply=%region_4.5 | all-reduce | flops 1 | bytes 8 | tf_op jit(solution)/shard_map/psum | solution.py:107
  (93 shorter events, 13.6 us)
Async XLA Ops:
  0.6 10.8 %copy-start.1 = (f32[4,2,32,8,128]{4,3,2,1,0:T(8,128)S(1)}, f32[4,2,32,8,128]{4,3,2,1,0:T(8,128)}, u32[]{:S(2)}) copy-start(f32[4,2,32,8,128]{4,3,2,1,0:T(8,128)} %param.6) | copy-start | bytes 3145732
  0.6 9.4 %copy-start.23 = (f32[8,128]{1,0:T(8,128)S(1)}, f32[8,128]{1,0:T(8,128)}, u32[]{:S(2)}) copy-start(f32[8,128]{1,0:T(8,128)} %param.9) | copy-start | bytes 12292
  0.7 10.0 %copy-start.28 = (s32[2]{0:T(128)S(1)}, s32[2]{0:T(128)}, u32[]{:S(2)}) copy-start(s32[2]{0:T(128)} %param.11) | copy-start | bytes 28
  0.7 10.0 %copy-start.19 = (s32[2,8,128]{2,1,0:T(8,128)S(1)}, s32[2,8,128]{2,1,0:T(8,128)}, u32[]{:S(2)}) copy-start(s32[2,8,128]{2,1,0:T(8,128)} %param.10) | copy-start | bytes 24580
  0.7 10.1 %copy-start.21 = (f32[2,8,128]{2,1,0:T(8,128)S(1)}, f32[2,8,128]{2,1,0:T(8,128)}, u32[]{:S(2)}) copy-start(f32[2,8,128]{2,1,0:T(8,128)} %param.8) | copy-start | bytes 24580
  2.9 12.0 %collective-permute-start.1 = (f32[4,2,32,2,128]{4,2,3,1,0:T(8,128)S(1)}, f32[4,2,32,2,128]{4,2,3,1,0:T(8,128)}, u32[]{:S(2)}, u32[]{:S(2)}) collective-permute-start(f32[4,2,32,2,128]{4,2,3,1,0:T(8,128)S(1)} %get-tuple-element.33), channel_id=1, source_target_pairs={{0,8},{8,16},{16,24},{24,32},{32,40},{40,48},{48,56},{56,64},{64,7... | collective-permute-start | bytes 786440 | tf_op jit(solution)/shard_map/ppermute | solution.py:26
  7.9 8.5 %collective-permute-start = (f32[4,2,32,2,128]{4,2,3,1,0:T(8,128)}, f32[4,2,32,2,128]{4,2,3,1,0:T(8,128)S(1)}, u32[]{:S(2)}, u32[]{:S(2)}) collective-permute-start(f32[4,2,32,2,128]{4,2,3,1,0:T(8,128)} %get-tuple-element.32), channel_id=1, source_target_pairs={{8,0},{16,8},{24,16},{32,24},{40,32},{48,40},{56,48},{64,56},{72,6... | collective-permute-start | bytes 786440 | tf_op jit(solution)/shard_map/ppermute | solution.py:27
  16.4 5.0 %copy-start.15 = (f32[4,2,32,2,128]{4,2,3,1,0:T(8,128)}, f32[4,2,32,2,128]{4,2,3,1,0:T(8,128)S(1)}, u32[]{:S(2)}) copy-start(f32[4,2,32,2,128]{4,2,3,1,0:T(8,128)S(1)} %collective-permute-done) | copy-start | bytes 786436
  21.4 9.9 %copy-start = (f32[4,2,32,12,128]{2,3,4,1,0:T(8,128)}, f32[4,2,32,12,128]{2,3,4,1,0:T(8,128)S(1)}, u32[]{:S(2)}) copy-start(f32[4,2,32,12,128]{2,3,4,1,0:T(8,128)S(1)} %pad_maximum_fusion) | copy-start | bytes 4718596
  22.1 16.3 %collective-permute-start.2 = (f32[4,2,32,12,2]{2,3,4,1,0:T(8,128)}, f32[4,2,32,12,2]{2,3,4,1,0:T(8,128)}, u32[]{:S(2)}, u32[]{:S(2)}) collective-permute-start(f32[4,2,32,12,2]{2,3,4,1,0:T(8,128)} %get-tuple-element.17), channel_id=1, source_target_pairs={{1,0},{2,1},{3,2},{4,3},{5,4},{6,5},{7,6},{9,8},{10,9},{11,10},{12... | collective-permute-start | bytes 73736 | tf_op jit(solution)/shard_map/ppermute | solution.py:27
  23.4 17.8 %collective-permute-start.3 = (f32[4,2,32,12,2]{2,3,4,1,0:T(8,128)S(1)}, f32[4,2,32,12,2]{2,3,4,1,0:T(8,128)}, u32[]{:S(2)}, u32[]{:S(2)}) collective-permute-start(f32[4,2,32,12,2]{2,3,4,1,0:T(8,128)S(1)} %get-tuple-element.16), channel_id=1, source_target_pairs={{0,1},{1,2},{2,3},{3,4},{4,5},{5,6},{6,7},{8,9},{9,10},{10,11},{11... | collective-permute-start | bytes 73736 | tf_op jit(solution)/shard_map/ppermute | solution.py:26
  43.9 5.9 %copy-start.3 = (f32[4,2,32,10,128]{4,2,3,1,0:T(8,128)S(1)}, f32[4,2,32,10,128]{4,2,3,1,0:T(8,128)}, u32[]{:S(2)}) copy-start(f32[4,2,32,10,128]{4,2,3,1,0:T(8,128)} %copy-done.2) | copy-start | bytes 3932164
  43.9 5.9 %copy-start.4 = (f32[4,2,32,12,128]{4,2,3,1,0:T(8,128)S(1)}, f32[4,2,32,12,128]{4,2,3,1,0:T(8,128)}, u32[]{:S(2)}) copy-start(f32[4,2,32,12,128]{4,2,3,1,0:T(8,128)} %copy.197) | copy-start | bytes 4718596
  43.9 5.9 %copy-start.7 = (f32[4,2,32,12,2]{4,2,3,1,0:T(8,128)S(1)}, f32[4,2,32,12,2]{4,2,3,1,0:T(8,128)}, u32[]{:S(2)}) copy-start(f32[4,2,32,12,2]{4,2,3,1,0:T(8,128)} %copy.198) | copy-start | bytes 73732
  43.9 5.9 %copy-start.17 = (f32[2,8,128]{2,1,0:T(8,128)S(1)}, f32[2,8,128]{2,1,0:T(8,128)}, u32[]{:S(2)}) copy-start(f32[2,8,128]{2,1,0:T(8,128)} %get-tuple-element.37) | copy-start | bytes 24580
  43.9 5.9 %copy-start.18 = (f32[2,8,128]{2,1,0:T(8,128)S(1)}, f32[2,8,128]{2,1,0:T(8,128)}, u32[]{:S(2)}) copy-start(f32[2,8,128]{2,1,0:T(8,128)} %get-tuple-element.38) | copy-start | bytes 24580
  49.9 3.6 %copy-start.8 = (f32[4,2,32,8,128]{4,2,3,1,0:T(8,128)S(1)}, f32[4,2,32,8,128]{4,2,3,1,0:T(8,128)}, u32[]{:S(2)}) copy-start(f32[4,2,32,8,128]{4,2,3,1,0:T(8,128)} %broadcast_multiply_fusion.1) | copy-start | bytes 3145732
  49.9 3.6 %copy-start.14 = (f32[4,2,32,8,128]{4,2,3,1,0:T(8,128)S(1)}, f32[4,2,32,8,128]{4,2,3,1,0:T(8,128)}, u32[]{:S(2)}) copy-start(f32[4,2,32,8,128]{4,2,3,1,0:T(8,128)} %get-tuple-element.14) | copy-start | bytes 3145732
  55.2 8.0 %collective-permute-start.4 = (f32[4,2,32,2,128]{4,2,3,1,0:T(8,128)S(1)}, f32[4,2,32,2,128]{4,2,3,1,0:T(8,128)S(1)}, u32[]{:S(2)}, u32[]{:S(2)}) collective-permute-start(f32[4,2,32,2,128]{4,2,3,1,0:T(8,128)S(1)} %get-tuple-element.30), channel_id=1, source_target_pairs={{8,0},{16,8},{24,16},{32,24},{40,32},{48,40},{56,48},{64,56},{72,6... | collective-permute-start | bytes 786440 | tf_op jit(solution)/shard_map/ppermute | solution.py:27
  57.1 7.2 %collective-permute-start.5 = (f32[4,2,32,2,128]{4,2,3,1,0:T(8,128)S(1)}, f32[4,2,32,2,128]{4,2,3,1,0:T(8,128)S(1)}, u32[]{:S(2)}, u32[]{:S(2)}) collective-permute-start(f32[4,2,32,2,128]{4,2,3,1,0:T(8,128)S(1)} %get-tuple-element.31), channel_id=1, source_target_pairs={{0,8},{8,16},{16,24},{24,32},{32,40},{40,48},{48,56},{56,64},{64,7... | collective-permute-start | bytes 786440 | tf_op jit(solution)/shard_map/ppermute | solution.py:26
  68.8 9.3 %collective-permute-start.6 = (f32[4,2,32,12,2]{2,3,4,1,0:T(8,128)S(1)}, f32[4,2,32,12,2]{2,3,4,1,0:T(8,128)S(1)}, u32[]{:S(2)}, u32[]{:S(2)}) collective-permute-start(f32[4,2,32,12,2]{2,3,4,1,0:T(8,128)S(1)} %copy.218), channel_id=1, source_target_pairs={{1,0},{2,1},{3,2},{4,3},{5,4},{6,5},{7,6},{9,8},{10,9},{11,10},{12... | collective-permute-start | bytes 73736 | tf_op jit(solution)/shard_map/ppermute | solution.py:27
  72.4 5.6 %copy-start.13 = (f32[2,32,8,128]{3,1,2,0:T(8,128)S(1)}, f32[2,32,8,128]{3,1,2,0:T(8,128)}, u32[]{:S(2)}) copy-start(f32[2,32,8,128]{3,1,2,0:T(8,128)} %multiply_multiply_fusion) | copy-start | bytes 786436
  72.4 7.6 %collective-permute-start.7 = (f32[4,2,32,12,2]{2,3,4,1,0:T(8,128)S(1)}, f32[4,2,32,12,2]{2,3,4,1,0:T(8,128)S(1)}, u32[]{:S(2)}, u32[]{:S(2)}) collective-permute-start(f32[4,2,32,12,2]{2,3,4,1,0:T(8,128)S(1)} %copy.219), channel_id=1, source_target_pairs={{0,1},{1,2},{2,3},{3,4},{4,5},{5,6},{6,7},{8,9},{9,10},{10,11},{11... | collective-permute-start | bytes 73736 | tf_op jit(solution)/shard_map/ppermute | solution.py:26
  81.8 4.1 %copy-start.5 = (f32[4,2,32,12,2]{4,2,3,1,0:T(8,128)S(1)}, f32[4,2,32,12,2]{4,2,3,1,0:T(8,128)}, u32[]{:S(2)}) copy-start(f32[4,2,32,12,2]{4,2,3,1,0:T(8,128)} %copy.207) | copy-start | bytes 73732
  81.8 4.1 %copy-start.6 = (f32[4,2,32,12,2]{4,2,3,1,0:T(8,128)S(1)}, f32[4,2,32,12,2]{4,2,3,1,0:T(8,128)}, u32[]{:S(2)}) copy-start(f32[4,2,32,12,2]{4,2,3,1,0:T(8,128)} %copy.209) | copy-start | bytes 73732
  89.1 8.1 %copy-start.20 = (s32[2,8,128]{2,1,0:T(8,128)S(1)}, s32[2,8,128]{2,1,0:T(8,128)}, u32[]{:S(2)}) copy-start(s32[2,8,128]{2,1,0:T(8,128)} %param.10) | copy-start | bytes 24580
  89.1 8.1 %copy-start.22 = (f32[2,8,128]{2,1,0:T(8,128)S(1)}, f32[2,8,128]{2,1,0:T(8,128)}, u32[]{:S(2)}) copy-start(f32[2,8,128]{2,1,0:T(8,128)} %param.8) | copy-start | bytes 24580
  89.1 8.1 %copy-start.24 = (f32[8,128]{1,0:T(8,128)S(1)}, f32[8,128]{1,0:T(8,128)}, u32[]{:S(2)}) copy-start(f32[8,128]{1,0:T(8,128)} %param.9) | copy-start | bytes 12292
  89.1 8.1 %copy-start.25 = (f32[8,128]{1,0:T(8,128)S(1)}, f32[8,128]{1,0:T(8,128)}, u32[]{:S(2)}) copy-start(f32[8,128]{1,0:T(8,128)} %get-tuple-element.40) | copy-start | bytes 12292
  89.1 8.1 %copy-start.27 = (f32[2]{0:T(128)S(1)}, f32[2]{0:T(128)}, u32[]{:S(2)}) copy-start(f32[2]{0:T(128)} %copy-done.26) | copy-start | bytes 28
  89.6 7.0 %collective-permute-start.8 = (f32[2,2,128]{2,1,0:T(2,128)S(1)}, f32[2,2,128]{2,1,0:T(2,128)S(1)}, u32[]{:S(2)}, u32[]{:S(2)}) collective-permute-start(f32[2,2,128]{2,1,0:T(2,128)S(1)} %get-tuple-element.42), channel_id=1, source_target_pairs={{8,0},{16,8},{24,16},{32,24},{40,32},{48,40},{56,48},{64,56},{72,6... | collective-permute-start | bytes 6152 | tf_op jit(solution)/shard_map/ppermute | solution.py:27
  91.5 5.7 %collective-permute-start.9 = (f32[2,2,128]{2,1,0:T(2,128)S(1)}, f32[2,2,128]{2,1,0:T(2,128)S(1)}, u32[]{:S(2)}, u32[]{:S(2)}) collective-permute-start(f32[2,2,128]{2,1,0:T(2,128)S(1)} %get-tuple-element.43), channel_id=1, source_target_pairs={{0,8},{8,16},{16,24},{24,32},{32,40},{40,48},{48,56},{56,64},{64,7... | collective-permute-start | bytes 6152 | tf_op jit(solution)/shard_map/ppermute | solution.py:26
  (7 other events, 12.1 us)
where the time goes:
time: 194 us; the launch traced here: 193 us
  blocking collectives  92.1 us (47%)
  local copies, waits for them, and re-layouts  35.3 us (18%)
  starting transfers between devices  31.4 us (16%)
  other arithmetic  28.4 us (15%)
  waiting for transfers between devices  3.91 us (2%)
    psum x1, blocking collectives, on_device(): total = lax.psum(jnp.sum(wall_grad * wall_grad), ('roll', 'trans'))  92.1 us
    ppermute x5, starting transfers between devices, extended(): before = lax.ppermute(last, axis, up)  22.7 us
    unnamed x65, local copies, waits for them, and re-layouts  13.8 us
    ppermute x5, starting transfers between devices, extended(): after = lax.ppermute(leading, axis, down)  8.63 us
    div x2, other arithmetic, time_section(): (-along_y(2) + 8.0 * along_y(1) - 8.0 * along_y(-1) + along_y(-2)) / 12.0  7.83 us
    add x2, other arithmetic, time_section(): diffused = fluid_viscosity * (second_x + second_y) + film_coef * second_z  7.57 us
    concatenate x2, local copies, waits for them, and re-layouts, extended(): array = jnp.concatenate([before, array, after], axis=dim)  6.07 us
    ppermute x3, local copies, waits for them, and re-layouts, extended(): before = lax.ppermute(last, axis, up)  5.96 us
  transfers between devices with their start and end apart: 10, of which 3 were waited for; matrix products, arithmetic and copies ran while one was open for 13% of the time, Pallas kernels for 0%

commit v1 on v0

v1 whole, which is shorter than its diff:
```python
import jax
import jax.numpy as jnp
from jax import lax
from jax.experimental import pallas as pl
from jax.experimental.pallas import tpu as pltpu
from jax.sharding import PartitionSpec as P

VISCOSITY_PRESS = 0.3
VISCOSITY_TEMP = 0.5
THETA_STEP = 0.2
SOUND = 0.5
KAPPA = 0.6
HEATING = 0.3
COURANT = 0.8

MESH = pl.DeviceIdType.MESH
NC = 4
CASES = 2
NZ = 32
NX = 8
NY = 128
Z0 = 8
ZROWS = 48
ZT = NZ // 8
ZRING = 8
GROUPS = ((0, 3), (3, 1))

STEP, SLOPE, COUPLE, HEAT, A0, A1, A3, B0, B1, B3, C0, C1, C3 = range(13)
AROW = (A0, A1, A1, A3)
BROW = (B0, B1, B1, B3)
CROW = (C0, C1, C1, C3)


def kernel(
    adjoint, source, pressure, film, cavity, temp, out, wall,
    s0, s1, fin, src, coef, ysend, yleft, yright, mean, curv, mine, plane, mine2, ring,
    in_sem, src_sem, out_sem, xsend_sem, xrecv_sem, ysend_sem, yrecv_sem,
    msend_sem, mrecv_sem, rsend_sem, rrecv_sem,
):
    nr, nt = lax.axis_size("roll"), lax.axis_size("trans")
    r, t = lax.axis_index("roll"), lax.axis_index("trans")
    core = lax.rem(r, 2)
    z = lax.rem(r // 2, ZRING)
    g = r // (2 * ZRING)
    groups = nr // (2 * ZRING)
    plane_n = groups * 2 * nt
    cells = nr * NX * nt * NY

    def plane_peer(o):
        dt, dg, dc = o // (2 * groups), (o // 2) % groups, o % 2
        row = (lax.rem(g + dg, groups) * ZRING + z) * 2 + lax.rem(core + dc, 2)
        return (row, lax.rem(t + dt, nt))

    def ring_peer(o):
        return ((g * ZRING + lax.rem(z + o, ZRING)) * 2 + core, t)

    up = (lax.rem(r + 1, nr), t)
    down = (lax.rem(r + nr - 1, nr), t)
    right = (r, lax.rem(t + 1, nt))
    left = (r, lax.rem(t + nt - 1, nt))
    has_up, has_down = r < nr - 1, r > 0
    has_right, has_left = t < nt - 1, t > 0

    loads, src_loads = [], []
    for case in range(CASES):
        for x in range(NX):
            loads.append(pltpu.make_async_copy(
                adjoint.at[:, case, :, x, :], s0.at[case, :, 2 + x, Z0:Z0 + NZ, :], in_sem.at[case, x]))
            src_loads.append(pltpu.make_async_copy(
                source.at[:, case, :, x, :], src.at[case, :, x], src_sem.at[case, x]))
    for copy in loads:
        copy.start()
    for copy in src_loads:
        copy.start()

    barrier = pltpu.get_barrier_semaphore()
    for o in range(1, plane_n):
        pl.semaphore_signal(barrier, inc=1, device_id=plane_peer(o), device_id_type=MESH)
    for o in range(1, ZRING):
        pl.semaphore_signal(barrier, inc=1, device_id=ring_peer(o), device_id_type=MESH)
    for peer in (up, down):
        pl.semaphore_signal(barrier, inc=1, device_id=peer, device_id_type=MESH)

    thick = film[...]
    for case in range(CASES):
        theta = THETA_STEP * temp[case].astype(jnp.float32)
        visc = jnp.exp(VISCOSITY_PRESS * pressure[case] - VISCOSITY_TEMP * theta)
        fcoef = 4.0 * visc / (thick * thick)
        density = 1.0 - 0.6 * cavity[case].astype(jnp.float32)
        step = COURANT / (32.0 / 3.0 * visc + 4.0 * fcoef + 2.0 * SOUND + 1.0)
        sv, sf = step * visc, step * fcoef
        rows = {
            STEP: step, SLOPE: step * density / 12.0, COUPLE: step * (SOUND / 12.0), HEAT: HEATING * sv,
        }
        for scale, a, b, c in ((0.5, A0, B0, C0), (1.0, A1, B1, C1), (KAPPA, A3, B3, C3)):
            rows[a] = (scale / 12.0) * sv
            rows[b] = scale * sf
            rows[c] = 1.0 - scale * (5.0 * sv + 2.0 * sf)
        for k, value in rows.items():
            coef[case, k] = value

    zero8 = jnp.zeros((8, NY), jnp.float32)
    for buf in (s0, s1):
        for case in range(CASES):
            def clear(i, _, buf=buf, case=case):
                for c in range(NC):
                    buf[case, c, i, 0:Z0, :] = zero8
                    buf[case, c, i, Z0 + NZ:ZROWS, :] = zero8
                return 0
            lax.fori_loop(0, NX + 4, clear, 0)
    for case in range(CASES):
        def clear(i, _, case=case):
            fin[case, i, 0:Z0, :] = zero8
            fin[case, i, Z0 + NZ:ZROWS, :] = zero8
            return 0
        lax.fori_loop(0, NX, clear, 0)

    def clear_slab(first):
        for buf in (s0, s1):
            for case in range(CASES):
                for c in range(NC):
                    for x in (first, first + 1):
                        buf[case, c, x, Z0:Z0 + NZ, :] = jnp.zeros((NZ, NY), jnp.float32)

    @pl.when(jnp.logical_not(has_down))
    def _():
        clear_slab(0)
        mean[0:2] = jnp.zeros((2, CASES, NY), jnp.float32)

    @pl.when(jnp.logical_not(has_up))
    def _():
        clear_slab(NX + 2)
        mean[NX + 2:NX + 4] = jnp.zeros((2, CASES, NY), jnp.float32)

    @pl.when(jnp.logical_not(has_left))
    def _():
        yleft[...] = jnp.zeros(yleft.shape, jnp.float32)

    @pl.when(jnp.logical_not(has_right))
    def _():
        yright[...] = jnp.zeros(yright.shape, jnp.float32)

    lane = lax.broadcasted_iota(jnp.int32, (8, NY), 1)
    sub = lax.broadcasted_iota(jnp.int32, (8, NY), 0)
    lane4 = lane // 4
    lo_half = lane % 4 < 2
    first1, first2, last1, last2 = lane == 0, lane < 2, lane == NY - 1, lane >= NY - 2
    heights = [(sub.astype(jnp.float32) + (8 * zt + 0.5)) / NZ for zt in range(ZT)]

    def x_copy(sec, grp, case, way):
        buf = (s0, s1)[sec]
        c, n = GROUPS[grp]
        a, b, peer = ((NX, 0, up), (2, NX + 2, down))[way]
        return pltpu.make_async_remote_copy(
            src_ref=buf.at[case, pl.ds(c, n), pl.ds(a, 2), pl.ds(Z0, NZ), :],
            dst_ref=buf.at[case, pl.ds(c, n), pl.ds(b, 2), pl.ds(Z0, NZ), :],
            send_sem=xsend_sem.at[sec, grp, case, way],
            recv_sem=xrecv_sem.at[sec, grp, case, way],
            device_id=peer, device_id_type=MESH)

    def y_copy(sec, grp, case, way):
        c, n = GROUPS[grp]
        dst, peer = ((yleft, right), (yright, left))[way]
        return pltpu.make_async_remote_copy(
            src_ref=ysend.at[sec, case, pl.ds(c, n)],
            dst_ref=dst.at[sec, case, pl.ds(c, n)],
            send_sem=ysend_sem.at[sec, grp, case, way],
            recv_sem=yrecv_sem.at[sec, grp, case, way],
            device_id=peer, device_id_type=MESH)

    def x_start(sec, grp, case):
        for way, ok in ((0, has_up), (1, has_down)):
            @pl.when(ok)
            def _(way=way):
                x_copy(sec, grp, case, way).start()

    def y_start(sec, grp, case):
        for way, ok in ((0, has_right), (1, has_left)):
            @pl.when(ok)
            def _(way=way):
                y_copy(sec, grp, case, way).start()

    def x_wait(sec, grp, case):
        for way, ok in ((0, has_down), (1, has_up)):
            @pl.when(ok)
            def _(way=way):
                x_copy(sec, grp, case, way).wait_recv()

    def y_wait(sec, grp, case):
        for way, ok in ((0, has_left), (1, has_right)):
            @pl.when(ok)
            def _(way=way):
                y_copy(sec, grp, case, way).wait_recv()

    def packed(acc, tile, q):
        return jnp.where(lane4 == q, pltpu.roll(tile, 4 * q + 2, 1), acc)

    def time_rows(sec, case, comps, first, count):
        buf = (s0, s1)[sec]

        def body(i, _):
            x = first + i

            def row(k):
                return jnp.broadcast_to(coef[case, k, pl.ds(x, 1), :], (8, NY))

            step, slope, couple = row(STEP), row(SLOPE), row(COUPLE)
            use_y = set(comps) | ({2} if 0 in comps else set()) | ({0} if 2 in comps else set())
            ghosts = {c: jnp.where(lo_half, yleft[sec, case, c], yright[sec, case, c]) for c in sorted(use_y)}
            packs = {}
            total = bend = None
            for zt in range(ZT):
                zs = Z0 + 8 * zt
                q = x * ZT + zt
                carry = slope * heights[zt]

                def at(c, dx=0, dz=0):
                    return buf[case, c, x + 2 + dx, zs + dz:zs + dz + 8, :]

                xd, yd, e1, e2 = {}, {}, {}, {}
                for c in sorted(set(comps) | ({1} if 0 in comps else set()) | ({0} if 1 in comps else set())):
                    p1, m1, p2, m2 = at(c, 1), at(c, -1), at(c, 2), at(c, -2)
                    xd[c] = 8.0 * (p1 - m1) - (p2 - m2)
                    e1[c], e2[c] = p1 + m1, p2 + m2
                for c in sorted(use_y):
                    f = at(c)
                    ghost = pltpu.roll(ghosts[c], NY - 2 - 4 * q, 1)
                    p1 = pltpu.roll(jnp.where(first1, ghost, f), NY - 1, 1)
                    p2 = pltpu.roll(jnp.where(first2, ghost, f), NY - 2, 1)
                    m1 = pltpu.roll(jnp.where(last1, ghost, f), 1, 1)
                    m2 = pltpu.roll(jnp.where(last2, ghost, f), 2, 1)
                    if c in (0, 2):
                        yd[c] = 8.0 * (p1 - m1) - (p2 - m2)
                    if c in comps:
                        e1[c], e2[c] = e1[c] + (p1 + m1), e2[c] + (p2 + m2)
                for c in comps:
                    f = at(c)
                    new = row(CROW[c]) * f + row(AROW[c]) * (16.0 * e1[c] - e2[c])
                    new = new + row(BROW[c]) * (at(c, 0, 1) + at(c, 0, -1))
                    new = new + (carry * xd[c] + step * src[case, c, x, 8 * zt:8 * zt + 8, :])
                    if c == 0:
                        new = new + couple * (xd[1] + yd[2])
                    elif c == 1:
                        new = new + couple * xd[0]
                    elif c == 2:
                        new = new + couple * yd[0]
                    else:
                        new = new + row(HEAT) * at(1)
                    if sec == 0:
                        s1[case, c, x + 2, zs:zs + 8, :] = new
                        packs[c] = packed(packs.get(c, ysend[1, case, c]), new, q)
                    else:
                        src[case, c, x, 8 * zt:8 * zt + 8, :] = new
                        if c == 1:
                            fin[case, x, zs:zs + 8, :] = new
                        if c == 0:
                            total = new if total is None else total + new
            for c, value in packs.items():
                ysend[1, case, c] = value
            if total is not None:
                mean[x + 2, case:case + 1, :] = jnp.sum(total, axis=0, keepdims=True)
            if sec == 1 and 1 in comps:
                for zt in range(ZT):
                    zs = Z0 + 8 * zt
                    f = fin[case, x, zs:zs + 8, :]
                    term = f * (fin[case, x, zs + 1:zs + 9, :] - 2.0 * f + fin[case, x, zs - 1:zs + 7, :])
                    bend = term if bend is None else bend + term
                curv[case, pl.ds(x, 1), :] = jnp.sum(bend, axis=0, keepdims=True)
            return 0

        lax.fori_loop(0, count, body, 0)

    for copy in loads:
        copy.wait()
    for case in range(CASES):
        for c in range(NC):
            ysend[1, case, c] = zero8
    for case in range(CASES):
        def pack_row(i, accs, case=case):
            accs = list(accs)
            for c in range(NC):
                for zt in range(ZT):
                    tile = s0[case, c, i + 2, Z0 + 8 * zt:Z0 + 8 * zt + 8, :]
                    accs[c] = packed(accs[c], tile, i * ZT + zt)
            return tuple(accs)
        accs = lax.fori_loop(0, NX, pack_row, (zero8,) * NC)
        for c in range(NC):
            ysend[0, case, c] = accs[c]
    pl.semaphore_wait(barrier, plane_n - 1 + ZRING - 1 + 2)
    for case in range(CASES):
        y_start(0, 0, case)
        x_start(0, 0, case)
    for case in range(CASES):
        y_start(0, 1, case)
        x_start(0, 1, case)

    for copy in src_loads:
        copy.wait()
    for case in range(CASES):
        y_wait(0, 0, case)
        time_rows(0, case, (0, 1, 2), 2, NX - 4)
    for case in range(CASES):
        x_wait(0, 0, case)
        time_rows(0, case, (0, 1, 2), 0, 2)
        time_rows(0, case, (0, 1, 2), NX - 2, 2)
        y_start(1, 0, case)
        x_start(1, 0, case)
    for case in range(CASES):
        y_wait(0, 1, case)
        x_wait(0, 1, case)
        time_rows(0, case, (3,), 0, NX)
        y_start(1, 1, case)
        x_start(1, 1, case)

    def store_out(c, case):
        copies = []
        for x in range(NX):
            copies.append(pltpu.make_async_copy(
                src.at[case, c, x], out.at[c, case, :, x, :], out_sem.at[c, case, x]))
        return copies

    for case in range(CASES):
        y_wait(1, 0, case)
        x_wait(1, 0, case)
        time_rows(1, case, (0,), 0, NX)

    def m_copy(way):
        a, b, peer = ((NX, 0, up), (2, NX + 2, down))[way]
        return pltpu.make_async_remote_copy(
            src_ref=mean.at[pl.ds(a, 2)], dst_ref=mean.at[pl.ds(b, 2)],
            send_sem=msend_sem.at[way], recv_sem=mrecv_sem.at[way],
            device_id=peer, device_id_type=MESH)

    for way, ok in ((0, has_up), (1, has_down)):
        @pl.when(ok)
        def _(way=way):
            m_copy(way).start()
    for case in range(CASES):
        time_rows(1, case, (1,), 0, NX)
        for c in (0, 1):
            for copy in store_out(c, case):
                copy.start()
    for way, ok in ((0, has_down), (1, has_up)):
        @pl.when(ok)
        def _(way=way):
            m_copy(way).wait_recv()

    grad = jnp.zeros((NX, NY), jnp.float32)
    for case in range(CASES):
        theta = THETA_STEP * temp[case].astype(jnp.float32)
        visc = jnp.exp(VISCOSITY_PRESS * pressure[case] - VISCOSITY_TEMP * theta)
        density = 1.0 - 0.6 * cavity[case].astype(jnp.float32)

        def rows(dx):
            return mean[2 + dx:2 + dx + NX, case, :]

        slope = (8.0 * (rows(1) - rows(-1)) - (rows(2) - rows(-2))) / (12.0 * NZ)
        grad = grad + (density * thick / 2.0 * slope
                       - 8.0 * visc / (thick * thick * thick) * (curv[case] / NZ))
    wall[...] = grad
    mine[0] = jnp.sum(grad * grad, axis=0, keepdims=True)

    def plane_copy(o):
        return pltpu.make_async_remote_copy(
            src_ref=mine.at[0], dst_ref=plane.at[o], send_sem=rsend_sem.at[0], recv_sem=rrecv_sem.at[0],
            device_id=plane_peer(o), device_id_type=MESH)

    def ring_copy(o):
        return pltpu.make_async_remote_copy(
            src_ref=mine2.at[0], dst_ref=ring.at[o], send_sem=rsend_sem.at[1], recv_sem=rrecv_sem.at[1],
            device_id=ring_peer(o), device_id_type=MESH)

    for o in range(1, plane_n):
        plane_copy(o).start()
    for case in range(CASES):
        time_rows(1, case, (2,), 0, NX)
    everyone = pltpu.make_async_copy(plane.at[pl.ds(1, plane_n - 1)], plane.at[pl.ds(1, plane_n - 1)], rrecv_sem.at[0])
    everyone.wait()
    mine2[0] = mine[0] + jnp.sum(plane[1:plane_n], axis=0)
    for o in range(1, ZRING):
        ring_copy(o).start()
    for case in range(CASES):
        for copy in store_out(2, case):
            copy.start()
    for case in range(CASES):
        y_wait(1, 1, case)
        x_wait(1, 1, case)
        time_rows(1, case, (3,), 0, NX)
        for copy in store_out(3, case):
            copy.start()
    pltpu.make_async_copy(ring.at[pl.ds(1, ZRING - 1)], ring.at[pl.ds(1, ZRING - 1)], rrecv_sem.at[1]).wait()
    total = jnp.sum(mine2[0] + jnp.sum(ring[1:ZRING], axis=0), axis=1, keepdims=True)
    wall[...] = wall[...] / jnp.sqrt(total / cells + 1e-06)

    pltpu.make_async_copy(plane.at[pl.ds(1, plane_n - 1)], plane.at[pl.ds(1, plane_n - 1)], rsend_sem.at[0]).wait()
    pltpu.make_async_copy(ring.at[pl.ds(1, ZRING - 1)], ring.at[pl.ds(1, ZRING - 1)], rsend_sem.at[1]).wait()
    for way, okx, oky in ((0, has_up, has_right), (1, has_down, has_left)):
        @pl.when(okx)
        def _(way=way):
            m_copy(way).wait_send()
            for sec in range(2):
                for grp in range(2):
                    for case in range(CASES):
                        x_copy(sec, grp, case, way).wait_send()

        @pl.when(oky)
        def _(way=way):
            for sec in range(2):
                for grp in range(2):
                    for case in range(CASES):
                        y_copy(sec, grp, case, way).wait_send()
    for c in range(NC):
        for case in range(CASES):
            for copy in store_out(c, case):
                copy.wait()


def on_device(adjoint, source, pressure, film, cavity, temp_index):
    vmem = pl.BlockSpec(memory_space=pltpu.VMEM)
    hbm = pl.BlockSpec(memory_space=pl.ANY)
    smem = pl.BlockSpec(memory_space=pltpu.SMEM)
    f32 = jnp.float32
    dma = pltpu.SemaphoreType.DMA
    return pl.pallas_call(
        kernel,
        out_shape=(
            jax.ShapeDtypeStruct(adjoint.shape, f32),
            jax.ShapeDtypeStruct(film.shape, f32),
        ),
        in_specs=[hbm, hbm, vmem, vmem, vmem, smem],
        out_specs=(hbm, vmem),
        scratch_shapes=[
            pltpu.VMEM((CASES, NC, NX + 4, ZROWS, NY), f32),
            pltpu.VMEM((CASES, NC, NX + 4, ZROWS, NY), f32),
            pltpu.VMEM((CASES, NX, ZROWS, NY), f32),
            pltpu.VMEM((CASES, NC, NX, NZ, NY), f32),
            pltpu.VMEM((CASES, 13, NX, NY), f32),
            pltpu.VMEM((2, CASES, NC, 8, NY), f32),
            pltpu.VMEM((2, CASES, NC, 8, NY), f32),
            pltpu.VMEM((2, CASES, NC, 8, NY), f32),
            pltpu.VMEM((NX + 4, CASES, NY), f32),
            pltpu.VMEM((CASES, NX, NY), f32),
            pltpu.VMEM((1, 1, NY), f32),
            pltpu.VMEM((32, 1, NY), f32),
            pltpu.VMEM((1, 1, NY), f32),
            pltpu.VMEM((ZRING, 1, NY), f32),
            dma((CASES, NX)),
            dma((CASES, NX)),
            dma((NC, CASES, NX)),
            dma((2, 2, CASES, 2)),
            dma((2, 2, CASES, 2)),
            dma((2, 2, CASES, 2)),
            dma((2, 2, CASES, 2)),
            dma((2,)),
            dma((2,)),
            dma((2,)),
            dma((2,)),
        ],
        compiler_params=pltpu.CompilerParams(
            collective_id=0, has_side_effects=True, vmem_limit_bytes=48 * 1024 * 1024
        ),
        name="lubrication_adjoint",
    )(adjoint, source, pressure, film, cavity, temp_index)


def solution(mesh):
    placed = (
        P(None, None, None, "roll", "trans"),
        P(None, None, None, "roll", "trans"),
        P(None, "roll", "trans"),
        P("roll", "trans"),
        P(None, "roll", "trans"),
        P(),
    )
    return jax.shard_map(
        on_device,
        mesh=mesh,
        in_specs=placed,
        out_specs=(P(None, None, None, "roll", "trans"), P("roll", "trans")),
        check_vma=False,
    )
```

time: 194 us -> 47.6 us (0.25)
  blocking collectives: 92.1 us -> 0 us
  Pallas kernels: 0 us -> 39.9 us
  starting transfers between devices: 31.4 us -> 0 us
  local copies, waits for them, and re-layouts: 35.3 us -> 6.74 us
  other arithmetic: 28.4 us -> 0 us
  waiting for transfers between devices: 3.91 us -> 0 us
    psum x1 -> x0, blocking collectives: 92.1 us -> none  [on_device(): total = lax.psum(jnp.sum(wall_grad * wall_grad), ('roll', 'trans'))]
    pallas_call x0 -> x1, Pallas kernels: none -> 39.9 us  [on_device(): pl.pallas_call(kernel, out_shape=(jax.ShapeDtypeStruct(adjoint.shape, f32...]
    ppermute x10 -> x0, starting transfers between devices: 31.4 us -> none  [the longest x5 22.7 us: extended(): before = lax.ppermute(last, axis, up)]
    ppermute x6 -> x0, local copies, waits for them, and re-layouts: 11.7 us -> none  [the longest x3 5.96 us: extended(): before = lax.ppermute(last, axis, up)]
    div x8 -> x0, other arithmetic: 11.7 us -> none  [the longest x2 7.83 us: time_section(): (-along_y(2) + 8.0 * along_y(1) - 8.0 * along_y(-1) + along_y(-2)) / 12.0]
    add x6 -> x0, other arithmetic: 9.29 us -> none  [the longest x2 7.57 us: time_section(): diffused = fluid_viscosity * (second_x + second_y) + film_coef * second_z]
    unnamed x65 -> x14, local copies, waits for them, and re-layouts: 13.8 us -> 6.74 us
    concatenate x2 -> x0, local copies, waits for them, and re-layouts: 6.07 us -> none  [extended(): array = jnp.concatenate([before, array, after], axis=dim)]
  transfers between devices with their start and end apart: 10 -> 0, of which waited for: 3 -> 0; matrix products, arithmetic and copies ran while one was open for 13% -> 0% of each run, Pallas kernels for 0% -> 0%
where the time goes in v1:
time: 47.6 us; the launch traced here: 47.3 us
  Pallas kernels  39.9 us (84%)
  local copies, waits for them, and re-layouts  6.74 us (14%)
  between operations  0.65 us (1%)
    pallas_call x1, Pallas kernels, on_device(): pl.pallas_call(kernel, out_shape=(jax.ShapeDtypeStruct(adjoint.shape, f32...  39.9 us
    unnamed x14, local copies, waits for them, and re-layouts  6.74 us

profile of v1, /device:TPU:1, one launch (start us, length us, event | category | flops | bytes accessed | tf_op | source)
XLA Modules:
  0.0 47.3 jit_solution(4031586526722225151)
XLA Ops:
  0.6 0.0 copy-start
  0.6 1.2 %copy-done = f32[4,2,32,8,128]{4,3,2,1,0:T(8,128)S(1)} copy-done((f32[4,2,32,8,128]{4,3,2,1,0:T(8,128)S(1)}, f32[4,2,32,8,128]{4,3,2,1,0:T(8,128)}, u32[]{:S(2)}) %copy-start) | copy-done | bytes 1048600
  1.9 0.0 copy-start.1
  1.9 1.2 %copy-done.1 = f32[4,2,32,8,128]{4,3,2,1,0:T(8,128)S(1)} copy-done((f32[4,2,32,8,128]{4,3,2,1,0:T(8,128)S(1)}, f32[4,2,32,8,128]{4,3,2,1,0:T(8,128)}, u32[]{:S(2)}) %copy-start.1) | copy-done | bytes 1048600
  3.1 0.0 copy-start.2
  3.1 0.7 %copy-done.2 = f32[2,8,128]{2,1,0:T(8,128)S(1)} copy-done((f32[2,8,128]{2,1,0:T(8,128)S(1)}, f32[2,8,128]{2,1,0:T(8,128)}, u32[]{:S(2)}) %copy-start.2) | copy-done | bytes 8216
  3.8 0.0 copy-start.3
  3.8 0.7 %copy-done.3 = s32[2,8,128]{2,1,0:T(8,128)S(1)} copy-done((s32[2,8,128]{2,1,0:T(8,128)S(1)}, s32[2,8,128]{2,1,0:T(8,128)}, u32[]{:S(2)}) %copy-start.3) | copy-done | bytes 8216
  4.5 0.0 copy-start.4
  4.5 0.7 %copy-done.4 = f32[8,128]{1,0:T(8,128)S(1)} copy-done((f32[8,128]{1,0:T(8,128)S(1)}, f32[8,128]{1,0:T(8,128)}, u32[]{:S(2)}) %copy-start.4) | copy-done | bytes 4120
  5.2 0.0 copy-start.5
  5.2 0.7 %copy-done.5 = s32[2]{0:T(128)S(1)} copy-done((s32[2]{0:T(128)S(1)}, s32[2]{0:T(128)}, u32[]{:S(2)}) %copy-start.5) | copy-done | bytes 32
  5.8 39.9 %lubrication_adjoint.1 = (f32[4,2,32,8,128]{4,3,2,1,0:T(8,128)S(1)}, f32[8,128]{1,0:T(8,128)S(1)}) custom-call(f32[4,2,32,8,128]{4,3,2,1,0:T(8,128)S(1)} %copy-done, f32[4,2,32,8,128]{4,3,2,1,0:T(8,128)S(1)} %copy-done.1, f32[2,8,128]{2,1,0:T(8,128)S(1)} %copy-done.2, f32[8,128]{1,0:T(8,128)S(1)} %copy-done.4, s32[2,8,128]{2,1,0:T(8,128)S(1)} %copy-done.3, ...), custom_call_target="tpu_custom_call" | custom-call | tf_op jit(solution)/shard_map/lubrication_adjoint/pallas_call | solution.py:424
  45.7 1.0 %copy.10 = f32[4,2,32,8,128]{4,3,2,1,0:T(8,128)} copy(f32[4,2,32,8,128]{4,3,2,1,0:T(8,128)S(1)} %get-tuple-element.4) | data formatting | bytes 2097152
  46.7 0.6 %copy.11 = f32[8,128]{1,0:T(8,128)} copy(f32[8,128]{1,0:T(8,128)S(1)} %get-tuple-element.5) | data formatting | bytes 8192
Async XLA Ops:
  0.6 1.2 %copy-start = (f32[4,2,32,8,128]{4,3,2,1,0:T(8,128)S(1)}, f32[4,2,32,8,128]{4,3,2,1,0:T(8,128)}, u32[]{:S(2)}) copy-start(f32[4,2,32,8,128]{4,3,2,1,0:T(8,128)} %adjoint.1) | copy-start | bytes 3145732
  1.9 1.2 %copy-start.1 = (f32[4,2,32,8,128]{4,3,2,1,0:T(8,128)S(1)}, f32[4,2,32,8,128]{4,3,2,1,0:T(8,128)}, u32[]{:S(2)}) copy-start(f32[4,2,32,8,128]{4,3,2,1,0:T(8,128)} %source.1) | copy-start | bytes 3145732
  3.1 0.7 %copy-start.2 = (f32[2,8,128]{2,1,0:T(8,128)S(1)}, f32[2,8,128]{2,1,0:T(8,128)}, u32[]{:S(2)}) copy-start(f32[2,8,128]{2,1,0:T(8,128)} %pressure.1) | copy-start | bytes 24580
  3.8 0.7 %copy-start.3 = (s32[2,8,128]{2,1,0:T(8,128)S(1)}, s32[2,8,128]{2,1,0:T(8,128)}, u32[]{:S(2)}) copy-start(s32[2,8,128]{2,1,0:T(8,128)} %cavity.1) | copy-start | bytes 24580
  4.5 0.7 %copy-start.4 = (f32[8,128]{1,0:T(8,128)S(1)}, f32[8,128]{1,0:T(8,128)}, u32[]{:S(2)}) copy-start(f32[8,128]{1,0:T(8,128)} %film.1) | copy-start | bytes 12292
  5.2 0.7 %copy-start.5 = (s32[2]{0:T(128)S(1)}, s32[2]{0:T(128)}, u32[]{:S(2)}) copy-start(s32[2]{0:T(128)} %temp.1) | copy-start | bytes 28

commit v2 on v1

--- a/solution.py
+++ b/solution.py
@@ -23,7 +23,8 @@
 ZROWS = 48
 ZT = NZ // 8
 ZRING = 8
-GROUPS = ((0, 3), (3, 1))
+XGROUPS = (((0, 3), (3, 1)), ((0, 2), (2, 2)))
+YGROUPS = (((0, 3), (3, 1)), ((0, 3), (3, 1)))
 
 STEP, SLOPE, COUPLE, HEAT, A0, A1, A3, B0, B1, B3, C0, C1, C3 = range(13)
 AROW = (A0, A1, A1, A3)
@@ -32,9 +33,10 @@
 
 
 def kernel(
-    adjoint, source, pressure, film, cavity, temp, out, wall,
+    adjoint, source, pressure_in, film_in, cavity_in, temp_in, out, wall,
+    pressure, film, cavity, temp,
     s0, s1, fin, src, coef, ysend, yleft, yright, mean, curv, mine, plane, mine2, ring,
-    in_sem, src_sem, out_sem, xsend_sem, xrecv_sem, ysend_sem, yrecv_sem,
+    small_sem, in_sem, src_sem, out_sem, xsend_sem, xrecv_sem, ysend_sem, yrecv_sem,
     msend_sem, mrecv_sem, rsend_sem, rrecv_sem,
 ):
     nr, nt = lax.axis_size("roll"), lax.axis_size("trans")
@@ -61,6 +63,21 @@
     has_up, has_down = r < nr - 1, r > 0
     has_right, has_left = t < nt - 1, t > 0
 
+    barrier = pltpu.get_barrier_semaphore()
+    for o in range(1, plane_n):
+        pl.semaphore_signal(barrier, inc=1, device_id=plane_peer(o), device_id_type=MESH)
+    for o in range(1, ZRING):
+        pl.semaphore_signal(barrier, inc=1, device_id=ring_peer(o), device_id_type=MESH)
+    for peer in (up, down):
+        pl.semaphore_signal(barrier, inc=1, device_id=peer, device_id_type=MESH)
+
+    smalls = [
+        pltpu.make_async_copy(given, held, small_sem.at[k])
+        for k, (given, held) in enumerate(
+            ((pressure_in, pressure), (film_in, film), (cavity_in, cavity), (temp_in, temp)))
+    ]
+    for copy in smalls:
+        copy.start()
     loads, src_loads = [], []
     for case in range(CASES):
         for x in range(NX):
@@ -73,14 +90,8 @@
     for copy in src_loads:
         copy.start()
 
-    barrier = pltpu.get_barrier_semaphore()
-    for o in range(1, plane_n):
-        pl.semaphore_signal(barrier, inc=1, device_id=plane_peer(o), device_id_type=MESH)
-    for o in range(1, ZRING):
-        pl.semaphore_signal(barrier, inc=1, device_id=ring_peer(o), device_id_type=MESH)
-    for peer in (up, down):
-        pl.semaphore_signal(barrier, inc=1, device_id=peer, device_id_type=MESH)
-
+    for copy in smalls:
+        copy.wait()
     thick = film[...]
     for case in range(CASES):
         theta = THETA_STEP * temp[case].astype(jnp.float32)
@@ -149,7 +160,7 @@
 
     def x_copy(sec, grp, case, way):
         buf = (s0, s1)[sec]
-        c, n = GROUPS[grp]
+        c, n = XGROUPS[sec][grp]
         a, b, peer = ((NX, 0, up), (2, NX + 2, down))[way]
         return pltpu.make_async_remote_copy(
             src_ref=buf.at[case, pl.ds(c, n), pl.ds(a, 2), pl.ds(Z0, NZ), :],
@@ -159,7 +170,7 @@
             device_id=peer, device_id_type=MESH)
 
     def y_copy(sec, grp, case, way):
-        c, n = GROUPS[grp]
+        c, n = YGROUPS[sec][grp]
         dst, peer = ((yleft, right), (yright, left))[way]
         return pltpu.make_async_remote_copy(
             src_ref=ysend.at[sec, case, pl.ds(c, n)],
@@ -290,9 +301,6 @@
     for case in range(CASES):
         y_start(0, 0, case)
         x_start(0, 0, case)
-    for case in range(CASES):
-        y_start(0, 1, case)
-        x_start(0, 1, case)
 
     for copy in src_loads:
         copy.wait()
@@ -306,11 +314,8 @@
         y_start(1, 0, case)
         x_start(1, 0, case)
     for case in range(CASES):
-        y_wait(0, 1, case)
-        x_wait(0, 1, case)
-        time_rows(0, case, (3,), 0, NX)
-        y_start(1, 1, case)
-        x_start(1, 1, case)
+        y_start(0, 1, case)
+        x_start(0, 1, case)
 
     def store_out(c, case):
         copies = []
@@ -373,21 +378,24 @@
     for o in range(1, plane_n):
         plane_copy(o).start()
     for case in range(CASES):
-        time_rows(1, case, (2,), 0, NX)
+        y_wait(0, 1, case)
+        x_wait(0, 1, case)
+        time_rows(0, case, (3,), 0, NX)
+        y_start(1, 1, case)
+        x_start(1, 1, case)
+
     everyone = pltpu.make_async_copy(plane.at[pl.ds(1, plane_n - 1)], plane.at[pl.ds(1, plane_n - 1)], rrecv_sem.at[0])
     everyone.wait()
     mine2[0] = mine[0] + jnp.sum(plane[1:plane_n], axis=0)
     for o in range(1, ZRING):
         ring_copy(o).start()
     for case in range(CASES):
-        for copy in store_out(2, case):
-            copy.start()
-    for case in range(CASES):
         y_wait(1, 1, case)
         x_wait(1, 1, case)
-        time_rows(1, case, (3,), 0, NX)
-        for copy in store_out(3, case):
-            copy.start()
+        time_rows(1, case, (2, 3), 0, NX)
+        for c in (2, 3):
+            for copy in store_out(c, case):
+                copy.start()
     pltpu.make_async_copy(ring.at[pl.ds(1, ZRING - 1)], ring.at[pl.ds(1, ZRING - 1)], rrecv_sem.at[1]).wait()
     total = jnp.sum(mine2[0] + jnp.sum(ring[1:ZRING], axis=0), axis=1, keepdims=True)
     wall[...] = wall[...] / jnp.sqrt(total / cells + 1e-06)
@@ -417,19 +425,23 @@
 
 def on_device(adjoint, source, pressure, film, cavity, temp_index):
     vmem = pl.BlockSpec(memory_space=pltpu.VMEM)
-    hbm = pl.BlockSpec(memory_space=pl.ANY)
-    smem = pl.BlockSpec(memory_space=pltpu.SMEM)
+    hbm = pl.BlockSpec(memory_space=pltpu.HBM)
     f32 = jnp.float32
     dma = pltpu.SemaphoreType.DMA
+    given = [
+        pltpu.with_memory_space_constraint(a, pltpu.HBM)
+        for a in (adjoint, source, pressure, film, cavity, temp_index)
+    ]
     return pl.pallas_call(
         kernel,
-        out_shape=(
-            jax.ShapeDtypeStruct(adjoint.shape, f32),
-            jax.ShapeDtypeStruct(film.shape, f32),
-        ),
-        in_specs=[hbm, hbm, vmem, vmem, vmem, smem],
-        out_specs=(hbm, vmem),
+        out_shape=(pltpu.VMEM(adjoint.shape, f32), pltpu.VMEM(film.shape, f32)),
+        in_specs=[hbm] * 6,
+        out_specs=(vmem, vmem),
         scratch_shapes=[
+            pltpu.VMEM(pressure.shape, f32),
+            pltpu.VMEM(film.shape, f32),
+            pltpu.VMEM(cavity.shape, jnp.int32),
+            pltpu.SMEM(temp_index.shape, jnp.int32),
             pltpu.VMEM((CASES, NC, NX + 4, ZROWS, NY), f32),
             pltpu.VMEM((CASES, NC, NX + 4, ZROWS, NY), f32),
             pltpu.VMEM((CASES, NX, ZROWS, NY), f32),
@@ -444,6 +456,7 @@
             pltpu.VMEM((32, 1, NY), f32),
             pltpu.VMEM((1, 1, NY), f32),
             pltpu.VMEM((ZRING, 1, NY), f32),
+            dma((4,)),
             dma((CASES, NX)),
             dma((CASES, NX)),
             dma((NC, CASES, NX)),
@@ -460,7 +473,7 @@
             collective_id=0, has_side_effects=True, vmem_limit_bytes=48 * 1024 * 1024
         ),
         name="lubrication_adjoint",
-    )(adjoint, source, pressure, film, cavity, temp_index)
+    )(*given)
 
 
 def solution(mesh):

time: 47.6 us -> 40.9 us (0.86)
  the two profiles are of different devices: /device:TPU:1 before, /device:TPU:24 now
where the time goes in v2:
time: 40.9 us; the launch traced here: 40.7 us
  Pallas kernels  38.5 us (94%)
  local copies, waits for them, and re-layouts  1.56 us (4%)
  between operations  0.64 us (2%)
    pallas_call x1, Pallas kernels, on_device(): pl.pallas_call(kernel, out_shape=(pltpu.VMEM(adjoint.shape, f32), pltpu.V...  38.5 us
    unnamed x2, local copies, waits for them, and re-layouts  1.56 us

profile of v2, /device:TPU:24, one launch (start us, length us, event | category | flops | bytes accessed | tf_op | source)
XLA Modules:
  0.0 40.7 jit_solution(1480011617893380215)
XLA Ops:
  0.6 38.5 %lubrication_adjoint.1 = (f32[4,2,32,8,128]{4,3,2,1,0:T(8,128)S(1)}, f32[8,128]{1,0:T(8,128)S(1)}) custom-call(f32[4,2,32,8,128]{4,3,2,1,0:T(8,128)} %adjoint.1, f32[4,2,32,8,128]{4,3,2,1,0:T(8,128)} %source.1, f32[2,8,128]{2,1,0:T(8,128)} %pressure_in.1, f32[8,128]{1,0:T(8,128)} %film_in.1, s32[2,8,128]{2,1,0:T(8,128)} %cavity_in.1, s32[2]{0:T(128)} %temp_in.1), custom_call_target="tpu_custom_call" | custom-call | tf_op jit(solution)/shard_map/lubrication_adjoint/pallas_call | solution.py:435
  39.2 1.0 %copy.10 = f32[4,2,32,8,128]{4,3,2,1,0:T(8,128)} copy(f32[4,2,32,8,128]{4,3,2,1,0:T(8,128)S(1)} %get-tuple-element.2) | data formatting | bytes 2097152
  40.2 0.6 %copy.11 = f32[8,128]{1,0:T(8,128)} copy(f32[8,128]{1,0:T(8,128)S(1)} %get-tuple-element.3) | data formatting | bytes 8192

commit v3 on v2

v3 whole, which is shorter than its diff:
```python
import jax
import jax.numpy as jnp
from jax import lax
from jax.experimental import pallas as pl
from jax.experimental.pallas import tpu as pltpu
from jax.sharding import PartitionSpec as P

VISCOSITY_PRESS = 0.3
VISCOSITY_TEMP = 0.5
THETA_STEP = 0.2
SOUND = 0.5
KAPPA = 0.6
HEATING = 0.3
COURANT = 0.8

MESH = pl.DeviceIdType.MESH
NC = 4
CASES = 2
NZ = 32
NX = 8
NY = 128
Z0 = 8
ZROWS = 48
ZT = NZ // 8
ZRING = 8
XGROUPS = (((0, 3), (3, 1)), ((0, 2), (2, 2)))
YGROUPS = (((0, 3), (3, 1)), ((0, 3), (3, 1)))

STEP, SLOPE, COUPLE, HEAT, A0, A1, A3, B0, B1, B3, C0, C1, C3 = range(13)
AROW = (A0, A1, A1, A3)
BROW = (B0, B1, B1, B3)
CROW = (C0, C1, C1, C3)


def kernel(
    adjoint, source, pressure_in, film_in, cavity_in, temp_in, out, wall,
    pressure, film, cavity, temp,
    s0, s1, halo, src, coef, pcoef, ysend, yleft, yright, mean, curv, mine, plane, mine2, ring,
    small_sem, in_sem, src_sem, out_sem, xsend_sem, xrecv_sem, ysend_sem, yrecv_sem,
    msend_sem, mrecv_sem, rsend_sem, rrecv_sem,
):
    nr, nt = lax.axis_size("roll"), lax.axis_size("trans")
    r, t = lax.axis_index("roll"), lax.axis_index("trans")
    core = lax.rem(r, 2)
    z = lax.rem(r // 2, ZRING)
    g = r // (2 * ZRING)
    groups = nr // (2 * ZRING)
    plane_n = groups * 2 * nt
    cells = nr * NX * nt * NY

    def plane_peer(o):
        dt, dg, dc = o // (2 * groups), (o // 2) % groups, o % 2
        row = (lax.rem(g + dg, groups) * ZRING + z) * 2 + lax.rem(core + dc, 2)
        return (row, lax.rem(t + dt, nt))

    def ring_peer(o):
        return ((g * ZRING + lax.rem(z + o, ZRING)) * 2 + core, t)

    up = (lax.rem(r + 1, nr), t)
    down = (lax.rem(r + nr - 1, nr), t)
    right = (r, lax.rem(t + 1, nt))
    left = (r, lax.rem(t + nt - 1, nt))
    has_up, has_down = r < nr - 1, r > 0
    has_right, has_left = t < nt - 1, t > 0

    barrier = pltpu.get_barrier_semaphore()
    for o in range(1, plane_n):
        pl.semaphore_signal(barrier, inc=1, device_id=plane_peer(o), device_id_type=MESH)
    for o in range(1, ZRING):
        pl.semaphore_signal(barrier, inc=1, device_id=ring_peer(o), device_id_type=MESH)
    for peer in (up, down):
        pl.semaphore_signal(barrier, inc=1, device_id=peer, device_id_type=MESH)

    smalls = [
        pltpu.make_async_copy(given, held, small_sem.at[k])
        for k, (given, held) in enumerate(
            ((pressure_in, pressure), (film_in, film), (cavity_in, cavity), (temp_in, temp)))
    ]
    loads = [
        pltpu.make_async_copy(
            adjoint.at[:, :, :, x, :], s0.at[:, :, 2 + x, pl.ds(Z0, NZ), :], in_sem.at[x])
        for x in range(NX)
    ]
    src_loads = [
        pltpu.make_async_copy(source.at[:, :, :, x, :], src.at[:, :, x], src_sem.at[x])
        for x in range(NX)
    ]
    for copy in smalls + loads + src_loads:
        copy.start()

    lane = lax.broadcasted_iota(jnp.int32, (8, NY), 1)
    sub = lax.broadcasted_iota(jnp.int32, (8, NY), 0)
    lane4, lane_in4 = lane // 4, lane % 4
    lo_half = lane_in4 < 2
    near1, near2 = lane_in4 == 1, lane_in4 == 2
    rim = jnp.logical_or(lane < 2, lane >= NY - 2)
    heights = [(sub.astype(jnp.float32) + (8 * zt + 0.5)) / NZ for zt in range(ZT)]
    zero8 = jnp.zeros((8, NY), jnp.float32)

    for buf in (s0, s1):
        def clear(i, _, buf=buf):
            for case in range(CASES):
                for c in range(NC):
                    buf[c, case, i, 0:Z0, :] = zero8
                    buf[c, case, i, Z0 + NZ:ZROWS, :] = zero8
            return 0
        lax.fori_loop(0, NX + 4, clear, 0)

        def clear_row(i, _, buf=buf):
            for case in range(CASES):
                for x in (0, 1, NX + 2, NX + 3):
                    for zt in range(ZT):
                        buf[i, case, x, Z0 + 8 * zt:Z0 + 8 * zt + 8, :] = zero8
            return 0
        lax.fori_loop(0, NC, clear_row, 0)

    def clear_pack(i, _):
        for case in range(CASES):
            for sec in range(2):
                ysend[sec, i, case] = zero8
        return 0
    lax.fori_loop(0, NC, clear_pack, 0)

    @pl.when(jnp.logical_not(has_down))
    def _():
        mean[0:2] = jnp.zeros((2, CASES, NY), jnp.float32)

    @pl.when(jnp.logical_not(has_up))
    def _():
        mean[NX + 2:NX + 4] = jnp.zeros((2, CASES, NY), jnp.float32)

    @pl.when(jnp.logical_not(has_left))
    def _():
        yleft[...] = jnp.zeros(yleft.shape, jnp.float32)

    @pl.when(jnp.logical_not(has_right))
    def _():
        yright[...] = jnp.zeros(yright.shape, jnp.float32)

    for copy in smalls:
        copy.wait()
    thick = film[...]
    for case in range(CASES):
        theta = THETA_STEP * temp[case].astype(jnp.float32)
        visc = jnp.exp(VISCOSITY_PRESS * pressure[case] - VISCOSITY_TEMP * theta)
        fcoef = 4.0 * visc / (thick * thick)
        density = 1.0 - 0.6 * cavity[case].astype(jnp.float32)
        step = COURANT / (32.0 / 3.0 * visc + 4.0 * fcoef + 2.0 * SOUND + 1.0)
        sv, sf = step * visc, step * fcoef
        table = {
            STEP: step, SLOPE: step * density / 12.0, COUPLE: step * (SOUND / 12.0), HEAT: HEATING * sv,
        }
        for scale, a, b, c in ((0.5, A0, B0, C0), (1.0, A1, B1, C1), (KAPPA, A3, B3, C3)):
            table[a] = (scale / 12.0) * sv
            table[b] = scale * sf
            table[c] = 1.0 - scale * (5.0 * sv + 2.0 * sf)
        for k, value in table.items():
            coef[case, k] = value
        for k, value in ((0, sv), (1, step)):
            acc = zero8
            for x in range(NX):
                here = jnp.logical_and(lane4 == ZT * x, sub == x)
                acc = jnp.where(here, pltpu.roll(value, 4 * ZT * x + 2, 1), acc)
            acc = acc + pltpu.roll(acc, 4, 1)
            acc = acc + pltpu.roll(acc, 8, 1)
            spread = jnp.broadcast_to(jnp.sum(acc, axis=0, keepdims=True), (8, NY))
            if k == 0:
                pcoef[case, 0] = (0.5 / 12.0) * spread
                pcoef[case, 1] = (1.0 / 12.0) * spread
                pcoef[case, 2] = (KAPPA / 12.0) * spread
            else:
                pcoef[case, 3] = (SOUND / 12.0) * spread

    def x_copy(sec, grp, case, way):
        buf = (s0, s1)[sec]
        c, n = XGROUPS[sec][grp]
        a, peer = ((NX, up), (2, down))[way]
        return pltpu.make_async_remote_copy(
            src_ref=buf.at[pl.ds(c, n), case, pl.ds(a, 2), pl.ds(Z0, NZ), :],
            dst_ref=halo.at[sec, way, case, pl.ds(c, n)],
            send_sem=xsend_sem.at[sec, grp, case, way],
            recv_sem=xrecv_sem.at[sec, grp, case, way],
            device_id=peer, device_id_type=MESH)

    def y_copy(sec, grp, case, way):
        c, n = YGROUPS[sec][grp]
        dst, peer = ((yleft, right), (yright, left))[way]
        return pltpu.make_async_remote_copy(
            src_ref=ysend.at[sec, pl.ds(c, n), case],
            dst_ref=dst.at[sec, pl.ds(c, n), case],
            send_sem=ysend_sem.at[sec, grp, case, way],
            recv_sem=yrecv_sem.at[sec, grp, case, way],
            device_id=peer, device_id_type=MESH)

    def x_start(sec, grp, case):
        for way, ok in ((0, has_up), (1, has_down)):
            @pl.when(ok)
            def _(way=way):
                x_copy(sec, grp, case, way).start()

    def y_start(sec, grp, case):
        for way, ok in ((0, has_right), (1, has_left)):
            @pl.when(ok)
            def _(way=way):
                y_copy(sec, grp, case, way).start()

    def y_wait(sec, grp, case):
        for way, ok in ((0, has_left), (1, has_right)):
            @pl.when(ok)
            def _(way=way):
                y_copy(sec, grp, case, way).wait_recv()

    def sent(copy, sec, grp, oks):
        for way in range(2):
            @pl.when(oks[way])
            def _(way=way):
                for case in range(CASES):
                    copy(sec, grp, case, way).wait_send()

    def row_of(case, k, x):
        return jnp.broadcast_to(coef[case, k, pl.ds(x, 1), :], (8, NY))

    def packed(acc, tile, q):
        return jnp.where(lane4 == q, pltpu.roll(tile, 4 * q + 2, 1), acc)

    def inner(sec, case, comps):
        cur, new_buf = ((s0, s1), (s1, s0))[sec]
        need_x = sorted(set(comps) | ({1} if 0 in comps else set()) | ({0} if 1 in comps else set()))
        need_y = sorted(set(comps) | ({2} if 0 in comps else set()) | ({0} if 2 in comps else set()))

        def body(x, _):
            def row(k):
                return row_of(case, k, x)

            step, slope, couple = row(STEP), row(SLOPE), row(COUPLE)
            packs = {}
            if sec == 0:
                packs = {(s, c): ysend[s, c, case] for c in comps for s in range(2)}
            for zt in range(ZT):
                zs = Z0 + 8 * zt
                q = x * ZT + zt
                carry = slope * heights[zt]

                def at(c, dx=0, dz=0):
                    return cur[c, case, x + 2 + dx, zs + dz:zs + dz + 8, :]

                xd, yd, e1, e2 = {}, {}, {}, {}
                for c in need_y:
                    f = at(c)
                    p1, m1 = pltpu.roll(f, NY - 1, 1), pltpu.roll(f, 1, 1)
                    p2, m2 = pltpu.roll(f, NY - 2, 1), pltpu.roll(f, 2, 1)
                    if (c == 2 and 0 in comps) or (c == 0 and 2 in comps):
                        yd[c] = 8.0 * (p1 - m1) - (p2 - m2)
                    e1[c], e2[c] = p1 + m1, p2 + m2
                    if sec == 0 and c in comps:
                        packs[0, c] = packed(packs[0, c], f, q)
                for c in need_x:
                    p1, m1, p2, m2 = at(c, 1), at(c, -1), at(c, 2), at(c, -2)
                    xd[c] = 8.0 * (p1 - m1) - (p2 - m2)
                    if c in comps:
                        e1[c], e2[c] = e1[c] + (p1 + m1), e2[c] + (p2 + m2)
                for c in comps:
                    new = row(CROW[c]) * at(c) + row(AROW[c]) * (16.0 * e1[c] - e2[c])
                    new = new + row(BROW[c]) * (at(c, 0, 1) + at(c, 0, -1))
                    new = new + (carry * xd[c] + step * src[c, case, x, 8 * zt:8 * zt + 8, :])
                    if c == 0:
                        new = new + couple * (xd[1] + yd[2])
                    elif c == 1:
                        new = new + couple * xd[0]
                    elif c == 2:
                        new = new + couple * yd[0]
                    else:
                        new = new + row(HEAT) * at(1)
                    new_buf[c, case, x + 2, zs:zs + 8, :] = new
                    if sec == 0:
                        packs[1, c] = packed(packs[1, c], new, q)
            for (s, c), value in packs.items():
                ysend[s, c, case] = value
            return 0

        lax.fori_loop(0, NX, body, 0)

    def rims(sec, case, comps):
        near, far, cross = {}, {}, {}
        for c in sorted(set(comps) | ({2} if 0 in comps else set()) | ({0} if 2 in comps else set())):
            d = jnp.where(lo_half, yleft[sec, c, case], yright[sec, c, case]) - ysend[sec, c, case]
            p1, m1 = pltpu.roll(d, NY - 1, 1), pltpu.roll(d, 1, 1)
            far_d = jnp.where(lo_half, pltpu.roll(d, NY - 2, 1), pltpu.roll(d, 2, 1))
            near[c] = 16.0 * jnp.where(near1, p1, jnp.where(near2, m1, 0.0)) - far_d
            cross[c] = 8.0 * jnp.where(near1, p1, jnp.where(near2, -m1, 0.0)) + jnp.where(lo_half, -far_d, far_d)
        result = {}
        for c in comps:
            value = pcoef[case, (0, 1, 1, 2)[c]] * near[c]
            if c in (0, 2):
                value = value + pcoef[case, 3] * cross[2 - c]
            result[c] = value
        return result

    def add_rims(sec, case, added, x):
        new_buf = (s1, s0)[sec]
        for c, value in added.items():
            for zt in range(ZT):
                zs = Z0 + 8 * zt
                here = jnp.where(rim, pltpu.roll(value, NY - 2 - 4 * (x * ZT + zt), 1), 0.0)
                new_buf[c, case, x + 2, zs:zs + 8, :] = new_buf[c, case, x + 2, zs:zs + 8, :] + here

    def edges(sec, grp, case, comps, wait=True):
        new_buf = (s1, s0)[sec]
        added = rims(sec, case, comps)
        for x in (0, 1, NX - 2, NX - 1):
            add_rims(sec, case, added, x)
        if sec == 0:
            for c in comps:
                ysend[1, c, case] = ysend[1, c, case] + added[c]
        for way, ok in ((0, has_down), (1, has_up)):
            @pl.when(ok)
            def _(way=way):
                if wait:
                    x_copy(sec, grp, case, way).wait_recv()
                packs = {c: zero8 for c in comps}
                outer, beside = ((0, 1), (NX - 1, NX - 2))[way]
                slopes = {x: row_of(case, SLOPE, x) for x in (outer, beside)}
                couples = {x: row_of(case, COUPLE, x) for x in (outer, beside)}
                for zt in range(ZT):
                    zs = Z0 + 8 * zt
                    h1, h2 = {}, {}
                    for c in sorted(set(comps) | ({1} if 0 in comps else set()) | ({0} if 1 in comps else set())):
                        first, second = ((1, 0), (0, 1))[way]
                        h1[c] = halo[sec, way, case, c, first, 8 * zt:8 * zt + 8, :]
                        h2[c] = halo[sec, way, case, c, second, 8 * zt:8 * zt + 8, :]
                    for x in (outer, beside):
                        carry = slopes[x] * heights[zt]
                        for c in comps:
                            mate = {0: 1, 1: 0}.get(c)
                            if x == outer:
                                lap = 16.0 * h1[c] - h2[c]
                                grad = lambda k: (h2[k] - 8.0 * h1[k]) if way == 0 else (8.0 * h1[k] - h2[k])
                            else:
                                lap = -h1[c]
                                grad = lambda k: h1[k] if way == 0 else -h1[k]
                            delta = row_of(case, AROW[c], x) * lap + carry * grad(c)
                            if mate is not None:
                                delta = delta + couples[x] * grad(mate)
                            new_buf[c, case, x + 2, zs:zs + 8, :] = new_buf[c, case, x + 2, zs:zs + 8, :] + delta
                            if sec == 0:
                                packs[c] = packed(packs[c], delta, x * ZT + zt)
                if sec == 0:
                    for c in comps:
                        ysend[1, c, case] = ysend[1, c, case] + packs[c]

    def middle(sec, case, comps):
        added = rims(sec, case, comps)

        def body(x, _):
            add_rims(sec, case, added, x)
            return 0

        lax.fori_loop(2, NX - 2, body, 0)

    for copy in loads + src_loads:
        copy.wait()
    for case in range(CASES):
        inner(0, case, (0, 1, 2))
    for case in range(CASES):
        inner(0, case, (3,))
    pl.semaphore_wait(barrier, plane_n - 1 + ZRING - 1 + 2)
    for case in range(CASES):
        y_start(0, 0, case)
        x_start(0, 0, case)
    for case in range(CASES):
        y_wait(0, 0, case)
        edges(0, 0, case, (0, 1, 2))
        y_start(1, 0, case)
        x_start(1, 0, case)
    for case in range(CASES):
        y_start(0, 1, case)
        x_start(0, 1, case)

    for case in range(CASES):
        middle(0, case, (0, 1, 2))
    sent(x_copy, 0, 0, (has_up, has_down))
    for case in range(CASES):
        inner(1, case, (0, 1))

    def mean_row(case, x):
        total = s0[0, case, x + 2, Z0:Z0 + 8, :]
        for zt in range(1, ZT):
            total = total + s0[0, case, x + 2, Z0 + 8 * zt:Z0 + 8 * zt + 8, :]
        mean[x + 2, case:case + 1, :] = jnp.sum(total, axis=0, keepdims=True)

    for case in range(CASES):
        y_wait(1, 0, case)
        edges(1, 0, case, (0,))
        for x in (0, 1, NX - 2, NX - 1):
            mean_row(case, x)

    def m_copy(way):
        a, b, peer = ((NX, 0, up), (2, NX + 2, down))[way]
        return pltpu.make_async_remote_copy(
            src_ref=mean.at[pl.ds(a, 2)], dst_ref=mean.at[pl.ds(b, 2)],
            send_sem=msend_sem.at[way], recv_sem=mrecv_sem.at[way],
            device_id=peer, device_id_type=MESH)

    for way, ok in ((0, has_up), (1, has_down)):
        @pl.when(ok)
        def _(way=way):
            m_copy(way).start()

    def store_out(c):
        return [
            pltpu.make_async_copy(
                s0.at[c, :, 2 + x, pl.ds(Z0, NZ), :], out.at[c, :, :, x, :], out_sem.at[c, x])
            for x in range(NX)
        ]

    for case in range(CASES):
        middle(1, case, (0,))

        def means(x, _, case=case):
            mean_row(case, x)
            return 0

        lax.fori_loop(2, NX - 2, means, 0)
        edges(1, 0, case, (1,), wait=False)
        middle(1, case, (1,))

        def bends(x, _, case=case):
            bend = None
            for zt in range(ZT):
                zs = Z0 + 8 * zt
                f = s0[1, case, x + 2, zs:zs + 8, :]
                term = f * (s0[1, case, x + 2, zs + 1:zs + 9, :] - 2.0 * f + s0[1, case, x + 2, zs - 1:zs + 7, :])
                bend = term if bend is None else bend + term
            curv[case, pl.ds(x, 1), :] = jnp.sum(bend, axis=0, keepdims=True)
            return 0

        lax.fori_loop(0, NX, bends, 0)
    for way, ok in ((0, has_down), (1, has_up)):
        @pl.when(ok)
        def _(way=way):
            m_copy(way).wait_recv()

    grad = jnp.zeros((NX, NY), jnp.float32)
    for case in range(CASES):
        theta = THETA_STEP * temp[case].astype(jnp.float32)
        visc = jnp.exp(VISCOSITY_PRESS * pressure[case] - VISCOSITY_TEMP * theta)
        density = 1.0 - 0.6 * cavity[case].astype(jnp.float32)

        def rows(dx):
            return mean[2 + dx:2 + dx + NX, case, :]

        slope = (8.0 * (rows(1) - rows(-1)) - (rows(2) - rows(-2))) / (12.0 * NZ)
        grad = grad + (density * thick / 2.0 * slope
                       - 8.0 * visc / (thick * thick * thick) * (curv[case] / NZ))
    wall[...] = grad
    mine[0] = jnp.sum(grad * grad, axis=0, keepdims=True)

    def plane_copy(o):
        return pltpu.make_async_remote_copy(
            src_ref=mine.at[0], dst_ref=plane.at[o], send_sem=rsend_sem.at[0], recv_sem=rrecv_sem.at[0],
            device_id=plane_peer(o), device_id_type=MESH)

    def ring_copy(o):
        return pltpu.make_async_remote_copy(
            src_ref=mine2.at[0], dst_ref=ring.at[o], send_sem=rsend_sem.at[1], recv_sem=rrecv_sem.at[1],
            device_id=ring_peer(o), device_id_type=MESH)

    for o in range(1, plane_n):
        plane_copy(o).start()

    for case in range(CASES):
        y_wait(0, 1, case)
        edges(0, 1, case, (3,))
        y_start(1, 1, case)
        x_start(1, 1, case)
    for c in (0, 1):
        for copy in store_out(c):
            copy.start()
    for case in range(CASES):
        middle(0, case, (3,))
    sent(x_copy, 0, 1, (has_up, has_down))
    pltpu.make_async_copy(plane.at[pl.ds(1, plane_n - 1)], plane.at[pl.ds(1, plane_n - 1)], rrecv_sem.at[0]).wait()
    mine2[0] = mine[0] + jnp.sum(plane[1:plane_n], axis=0)
    for o in range(1, ZRING):
        ring_copy(o).start()
    for case in range(CASES):
        inner(1, case, (2, 3))
    for case in range(CASES):
        y_wait(1, 1, case)
        edges(1, 1, case, (2, 3))
        middle(1, case, (2, 3))
    for c in (2, 3):
        for copy in store_out(c):
            copy.start()
    pltpu.make_async_copy(ring.at[pl.ds(1, ZRING - 1)], ring.at[pl.ds(1, ZRING - 1)], rrecv_sem.at[1]).wait()
    total = jnp.sum(mine2[0] + jnp.sum(ring[1:ZRING], axis=0), axis=1, keepdims=True)
    wall[...] = wall[...] / jnp.sqrt(total / cells + 1e-06)

    pltpu.make_async_copy(plane.at[pl.ds(1, plane_n - 1)], plane.at[pl.ds(1, plane_n - 1)], rsend_sem.at[0]).wait()
    pltpu.make_async_copy(ring.at[pl.ds(1, ZRING - 1)], ring.at[pl.ds(1, ZRING - 1)], rsend_sem.at[1]).wait()
    for way, ok in ((0, has_up), (1, has_down)):
        @pl.when(ok)
        def _(way=way):
            m_copy(way).wait_send()
    for grp in range(2):
        sent(x_copy, 1, grp, (has_up, has_down))
        for sec in range(2):
            sent(y_copy, sec, grp, (has_right, has_left))
    for c in range(NC):
        for copy in store_out(c):
            copy.wait()


def on_device(adjoint, source, pressure, film, cavity, temp_index):
    vmem = pl.BlockSpec(memory_space=pltpu.VMEM)
    hbm = pl.BlockSpec(memory_space=pltpu.HBM)
    f32 = jnp.float32
    dma = pltpu.SemaphoreType.DMA
    given = [
        pltpu.with_memory_space_constraint(a, pltpu.HBM)
        for a in (adjoint, source, pressure, film, cavity, temp_index)
    ]
    return pl.pallas_call(
        kernel,
        out_shape=(pltpu.VMEM(adjoint.shape, f32), pltpu.VMEM(film.shape, f32)),
        in_specs=[hbm] * 6,
        out_specs=(vmem, vmem),
        scratch_shapes=[
            pltpu.VMEM(pressure.shape, f32),
            pltpu.VMEM(film.shape, f32),
            pltpu.VMEM(cavity.shape, jnp.int32),
            pltpu.SMEM(temp_index.shape, jnp.int32),
            pltpu.VMEM((NC, CASES, NX + 4, ZROWS, NY), f32),
            pltpu.VMEM((NC, CASES, NX + 4, ZROWS, NY), f32),
            pltpu.VMEM((2, 2, CASES, NC, 2, NZ, NY), f32),
            pltpu.VMEM((NC, CASES, NX, NZ, NY), f32),
            pltpu.VMEM((CASES, 13, NX, NY), f32),
            pltpu.VMEM((CASES, 4, 8, NY), f32),
            pltpu.VMEM((2, NC, CASES, 8, NY), f32),
            pltpu.VMEM((2, NC, CASES, 8, NY), f32),
            pltpu.VMEM((2, NC, CASES, 8, NY), f32),
            pltpu.VMEM((NX + 4, CASES, NY), f32),
            pltpu.VMEM((CASES, NX, NY), f32),
            pltpu.VMEM((1, 1, NY), f32),
            pltpu.VMEM((32, 1, NY), f32),
            pltpu.VMEM((1, 1, NY), f32),
            pltpu.VMEM((ZRING, 1, NY), f32),
            dma((4,)),
            dma((NX,)),
            dma((NX,)),
            dma((NC, NX)),
            dma((2, 2, CASES, 2)),
            dma((2, 2, CASES, 2)),
            dma((2, 2, CASES, 2)),
            dma((2, 2, CASES, 2)),
            dma((2,)),
            dma((2,)),
            dma((2,)),
            dma((2,)),
        ],
        compiler_params=pltpu.CompilerParams(
            collective_id=0, has_side_effects=True, vmem_limit_bytes=48 * 1024 * 1024
        ),
        name="lubrication_adjoint",
    )(*given)


def solution(mesh):
    placed = (
        P(None, None, None, "roll", "trans"),
        P(None, None, None, "roll", "trans"),
        P(None, "roll", "trans"),
        P("roll", "trans"),
        P(None, "roll", "trans"),
        P(),
    )
    return jax.shard_map(
        on_device,
        mesh=mesh,
        in_specs=placed,
        out_specs=(P(None, None, None, "roll", "trans"), P("roll", "trans")),
        check_vma=False,
    )
```

time: 40.9 us -> 39.5 us (0.966)
  the two profiles are of different devices: /device:TPU:24 before, /device:TPU:1 now
where the time goes in v3:
time: 39.5 us; the launch traced here: 39.4 us
  Pallas kernels  37.2 us (94%)
  local copies, waits for them, and re-layouts  1.56 us (4%)
  between operations  0.64 us (2%)
    pallas_call x1, Pallas kernels, on_device(): pl.pallas_call(kernel, out_shape=(pltpu.VMEM(adjoint.shape, f32), pltpu.V...  37.2 us
    unnamed x2, local copies, waits for them, and re-layouts  1.56 us

profile of v3, /device:TPU:1, one launch (start us, length us, event | category | flops | bytes accessed | tf_op | source)
XLA Modules:
  0.0 39.4 jit_solution(9914242309323508365)
XLA Ops:
  0.6 37.2 %lubrication_adjoint.1 = (f32[4,2,32,8,128]{4,3,2,1,0:T(8,128)S(1)}, f32[8,128]{1,0:T(8,128)S(1)}) custom-call(f32[4,2,32,8,128]{4,3,2,1,0:T(8,128)} %adjoint.1, f32[4,2,32,8,128]{4,3,2,1,0:T(8,128)} %source.1, f32[2,8,128]{2,1,0:T(8,128)} %pressure_in.1, f32[8,128]{1,0:T(8,128)} %film_in.1, s32[2,8,128]{2,1,0:T(8,128)} %cavity_in.1, s32[2]{0:T(128)} %temp_in.1), custom_call_target="tpu_custom_call" | custom-call | tf_op jit(solution)/shard_map/lubrication_adjoint/pallas_call | solution.py:523
  37.8 1.0 %copy.10 = f32[4,2,32,8,128]{4,3,2,1,0:T(8,128)} copy(f32[4,2,32,8,128]{4,3,2,1,0:T(8,128)S(1)} %get-tuple-element.2) | data formatting | bytes 2097152
  38.8 0.6 %copy.11 = f32[8,128]{1,0:T(8,128)} copy(f32[8,128]{1,0:T(8,128)S(1)} %get-tuple-element.3) | data formatting | bytes 8192

commit v4 on v3

--- a/solution.py
+++ b/solution.py
@@ -23,7 +23,7 @@
 ZROWS = 48
 ZT = NZ // 8
 ZRING = 8
-XGROUPS = (((0, 3), (3, 1)), ((0, 2), (2, 2)))
+XGROUPS = (((0, 3), (3, 1)), ((0, 2), (2, 1), (3, 1)))
 YGROUPS = (((0, 3), (3, 1)), ((0, 3), (3, 1)))
 
 STEP, SLOPE, COUPLE, HEAT, A0, A1, A3, B0, B1, B3, C0, C1, C3 = range(13)
@@ -36,7 +36,7 @@
     adjoint, source, pressure_in, film_in, cavity_in, temp_in, out, wall,
     pressure, film, cavity, temp,
     s0, s1, halo, src, coef, pcoef, ysend, yleft, yright, mean, curv, mine, plane, mine2, ring,
-    small_sem, in_sem, src_sem, out_sem, xsend_sem, xrecv_sem, ysend_sem, yrecv_sem,
+    small_sem, in_sem, out_sem, xsend_sem, xrecv_sem, ysend_sem, yrecv_sem,
     msend_sem, mrecv_sem, rsend_sem, rrecv_sem,
 ):
     nr, nt = lax.axis_size("roll"), lax.axis_size("trans")
@@ -78,11 +78,11 @@
     ]
     loads = [
         pltpu.make_async_copy(
-            adjoint.at[:, :, :, x, :], s0.at[:, :, 2 + x, pl.ds(Z0, NZ), :], in_sem.at[x])
+            adjoint.at[:, :, :, x, :], s0.at[:, :, 2 + x, pl.ds(Z0, NZ), :], in_sem.at[0])
         for x in range(NX)
     ]
     src_loads = [
-        pltpu.make_async_copy(source.at[:, :, :, x, :], src.at[:, :, x], src_sem.at[x])
+        pltpu.make_async_copy(source.at[:, :, :, x, :], src.at[:, :, x], in_sem.at[1])
         for x in range(NX)
     ]
     for copy in smalls + loads + src_loads:
@@ -116,8 +116,7 @@
 
     def clear_pack(i, _):
         for case in range(CASES):
-            for sec in range(2):
-                ysend[sec, i, case] = zero8
+            ysend[1, i, case] = zero8
         return 0
     lax.fori_loop(0, NC, clear_pack, 0)
 
@@ -178,7 +177,7 @@
         return pltpu.make_async_remote_copy(
             src_ref=buf.at[pl.ds(c, n), case, pl.ds(a, 2), pl.ds(Z0, NZ), :],
             dst_ref=halo.at[sec, way, case, pl.ds(c, n)],
-            send_sem=xsend_sem.at[sec, grp, case, way],
+            send_sem=xsend_sem.at[sec, grp, way],
             recv_sem=xrecv_sem.at[sec, grp, case, way],
             device_id=peer, device_id_type=MESH)
 
@@ -188,7 +187,7 @@
         return pltpu.make_async_remote_copy(
             src_ref=ysend.at[sec, pl.ds(c, n), case],
             dst_ref=dst.at[sec, pl.ds(c, n), case],
-            send_sem=ysend_sem.at[sec, grp, case, way],
+            send_sem=ysend_sem.at[sec, way],
             recv_sem=yrecv_sem.at[sec, grp, case, way],
             device_id=peer, device_id_type=MESH)
 
@@ -210,12 +209,19 @@
             def _(way=way):
                 y_copy(sec, grp, case, way).wait_recv()
 
-    def sent(copy, sec, grp, oks):
-        for way in range(2):
-            @pl.when(oks[way])
+    def x_sent(sec, grp):
+        c, n = XGROUPS[sec][grp]
+        for way, ok in ((0, has_up), (1, has_down)):
+            @pl.when(ok)
             def _(way=way):
-                for case in range(CASES):
-                    copy(sec, grp, case, way).wait_send()
+                both = halo.at[sec, way, :, pl.ds(c, n)]
+                pltpu.make_async_copy(both, both, xsend_sem.at[sec, grp, way]).wait()
+
+    def y_sent(sec):
+        for way, ok in ((0, has_right), (1, has_left)):
+            @pl.when(ok)
+            def _(way=way):
+                pltpu.make_async_copy(ysend.at[sec], ysend.at[sec], ysend_sem.at[sec, way]).wait()
 
     def row_of(case, k, x):
         return jnp.broadcast_to(coef[case, k, pl.ds(x, 1), :], (8, NY))
@@ -235,7 +241,7 @@
             step, slope, couple = row(STEP), row(SLOPE), row(COUPLE)
             packs = {}
             if sec == 0:
-                packs = {(s, c): ysend[s, c, case] for c in comps for s in range(2)}
+                packs = {c: ysend[1, c, case] for c in comps}
             for zt in range(ZT):
                 zs = Z0 + 8 * zt
                 q = x * ZT + zt
@@ -252,8 +258,6 @@
                     if (c == 2 and 0 in comps) or (c == 0 and 2 in comps):
                         yd[c] = 8.0 * (p1 - m1) - (p2 - m2)
                     e1[c], e2[c] = p1 + m1, p2 + m2
-                    if sec == 0 and c in comps:
-                        packs[0, c] = packed(packs[0, c], f, q)
                 for c in need_x:
                     p1, m1, p2, m2 = at(c, 1), at(c, -1), at(c, 2), at(c, -2)
                     xd[c] = 8.0 * (p1 - m1) - (p2 - m2)
@@ -273,12 +277,12 @@
                         new = new + row(HEAT) * at(1)
                     new_buf[c, case, x + 2, zs:zs + 8, :] = new
                     if sec == 0:
-                        packs[1, c] = packed(packs[1, c], new, q)
-            for (s, c), value in packs.items():
-                ysend[s, c, case] = value
+                        packs[c] = packed(packs[c], new, q)
+            for c, value in packs.items():
+                ysend[1, c, case] = value
             return 0
 
-        lax.fori_loop(0, NX, body, 0)
+        lax.fori_loop(0, NX, body, 0, unroll=2)
 
     def rims(sec, case, comps):
         near, far, cross = {}, {}, {}
@@ -304,7 +308,7 @@
                 here = jnp.where(rim, pltpu.roll(value, NY - 2 - 4 * (x * ZT + zt), 1), 0.0)
                 new_buf[c, case, x + 2, zs:zs + 8, :] = new_buf[c, case, x + 2, zs:zs + 8, :] + here
 
-    def edges(sec, grp, case, comps, wait=True):
+    def edges(sec, grps, case, comps):
         new_buf = (s1, s0)[sec]
         added = rims(sec, case, comps)
         for x in (0, 1, NX - 2, NX - 1):
@@ -315,7 +319,7 @@
         for way, ok in ((0, has_down), (1, has_up)):
             @pl.when(ok)
             def _(way=way):
-                if wait:
+                for grp in grps:
                     x_copy(sec, grp, case, way).wait_recv()
                 packs = {c: zero8 for c in comps}
                 outer, beside = ((0, 1), (NX - 1, NX - 2))[way]
@@ -357,28 +361,40 @@
 
         lax.fori_loop(2, NX - 2, body, 0)
 
-    for copy in loads + src_loads:
-        copy.wait()
+    pltpu.make_async_copy(adjoint, adjoint, in_sem.at[0]).wait()
+    for case in range(CASES):
+        def pack_rows(x, accs, case=case):
+            accs = list(accs)
+            for c in range(NC):
+                for zt in range(ZT):
+                    accs[c] = packed(accs[c], s0[c, case, x + 2, Z0 + 8 * zt:Z0 + 8 * zt + 8, :], x * ZT + zt)
+            return tuple(accs)
+
+        accs = lax.fori_loop(0, NX, pack_rows, (zero8,) * NC)
+        for c in range(NC):
+            ysend[0, c, case] = accs[c]
+    pl.semaphore_wait(barrier, plane_n - 1 + ZRING - 1 + 2)
+    for case in range(CASES):
+        x_start(0, 0, case)
+        y_start(0, 0, case)
+    pltpu.make_async_copy(source, source, in_sem.at[1]).wait()
     for case in range(CASES):
         inner(0, case, (0, 1, 2))
     for case in range(CASES):
-        inner(0, case, (3,))
-    pl.semaphore_wait(barrier, plane_n - 1 + ZRING - 1 + 2)
-    for case in range(CASES):
-        y_start(0, 0, case)
-        x_start(0, 0, case)
-    for case in range(CASES):
         y_wait(0, 0, case)
-        edges(0, 0, case, (0, 1, 2))
+        edges(0, (0,), case, (0, 1, 2))
         y_start(1, 0, case)
         x_start(1, 0, case)
     for case in range(CASES):
         y_start(0, 1, case)
         x_start(0, 1, case)
+        x_start(1, 1, case)
 
     for case in range(CASES):
         middle(0, case, (0, 1, 2))
-    sent(x_copy, 0, 0, (has_up, has_down))
+    x_sent(0, 0)
+    for case in range(CASES):
+        inner(0, case, (3,))
     for case in range(CASES):
         inner(1, case, (0, 1))
 
@@ -390,7 +406,7 @@
 
     for case in range(CASES):
         y_wait(1, 0, case)
-        edges(1, 0, case, (0,))
+        edges(1, (0,), case, (0,))
         for x in (0, 1, NX - 2, NX - 1):
             mean_row(case, x)
 
@@ -406,10 +422,16 @@
         def _(way=way):
             m_copy(way).start()
 
+    for case in range(CASES):
+        y_wait(0, 1, case)
+        edges(0, (1,), case, (3,))
+        y_start(1, 1, case)
+        x_start(1, 2, case)
+
     def store_out(c):
         return [
             pltpu.make_async_copy(
-                s0.at[c, :, 2 + x, pl.ds(Z0, NZ), :], out.at[c, :, :, x, :], out_sem.at[c, x])
+                s0.at[c, :, 2 + x, pl.ds(Z0, NZ), :], out.at[c, :, :, x, :], out_sem.at[c])
             for x in range(NX)
         ]
 
@@ -421,7 +443,7 @@
             return 0
 
         lax.fori_loop(2, NX - 2, means, 0)
-        edges(1, 0, case, (1,), wait=False)
+        edges(1, (), case, (1,))
         middle(1, case, (1,))
 
         def bends(x, _, case=case):
@@ -465,29 +487,28 @@
             src_ref=mine2.at[0], dst_ref=ring.at[o], send_sem=rsend_sem.at[1], recv_sem=rrecv_sem.at[1],
             device_id=ring_peer(o), device_id_type=MESH)
 
-    for o in range(1, plane_n):
+    def hops(o):
+        dt = o // (2 * groups)
+        return min(dt % 4, 4 - dt % 4) + 2 * (dt >= 4) + (o // 2) % groups
+
+    for o in sorted(range(1, plane_n), key=lambda o: -hops(o)):
         plane_copy(o).start()
 
-    for case in range(CASES):
-        y_wait(0, 1, case)
-        edges(0, 1, case, (3,))
-        y_start(1, 1, case)
-        x_start(1, 1, case)
     for c in (0, 1):
         for copy in store_out(c):
             copy.start()
     for case in range(CASES):
         middle(0, case, (3,))
-    sent(x_copy, 0, 1, (has_up, has_down))
+    x_sent(0, 1)
+    for case in range(CASES):
+        inner(1, case, (2, 3))
     pltpu.make_async_copy(plane.at[pl.ds(1, plane_n - 1)], plane.at[pl.ds(1, plane_n - 1)], rrecv_sem.at[0]).wait()
     mine2[0] = mine[0] + jnp.sum(plane[1:plane_n], axis=0)
-    for o in range(1, ZRING):
+    for o in sorted(range(1, ZRING), key=lambda o: -min(o, ZRING - o)):
         ring_copy(o).start()
     for case in range(CASES):
-        inner(1, case, (2, 3))
-    for case in range(CASES):
         y_wait(1, 1, case)
-        edges(1, 1, case, (2, 3))
+        edges(1, (1, 2), case, (2, 3))
         middle(1, case, (2, 3))
     for c in (2, 3):
         for copy in store_out(c):
@@ -502,13 +523,12 @@
         @pl.when(ok)
         def _(way=way):
             m_copy(way).wait_send()
-    for grp in range(2):
-        sent(x_copy, 1, grp, (has_up, has_down))
-        for sec in range(2):
-            sent(y_copy, sec, grp, (has_right, has_left))
+    for grp in range(3):
+        x_sent(1, grp)
+    for sec in range(2):
+        y_sent(sec)
     for c in range(NC):
-        for copy in store_out(c):
-            copy.wait()
+        pltpu.make_async_copy(out.at[c], out.at[c], out_sem.at[c]).wait()
 
 
 def on_device(adjoint, source, pressure, film, cavity, temp_index):
@@ -546,12 +566,11 @@
             pltpu.VMEM((1, 1, NY), f32),
             pltpu.VMEM((ZRING, 1, NY), f32),
             dma((4,)),
-            dma((NX,)),
-            dma((NX,)),
-            dma((NC, NX)),
-            dma((2, 2, CASES, 2)),
-            dma((2, 2, CASES, 2)),
-            dma((2, 2, CASES, 2)),
+            dma((2,)),
+            dma((NC,)),
+            dma((2, 3, 2)),
+            dma((2, 3, CASES, 2)),
+            dma((2, 2)),
             dma((2, 2, CASES, 2)),
             dma((2,)),
             dma((2,)),

time: 39.5 us -> 34.1 us (0.86)
  Pallas kernels: 37.2 us -> 31.8 us
    pallas_call x1, Pallas kernels: 37.2 us -> 31.8 us  [on_device(): pl.pallas_call(kernel, out_shape=(pltpu.VMEM(adjoint.shape, f32), pltpu.V...]
where the time goes in v4:
time: 34.1 us; the launch traced here: 34 us
  Pallas kernels  31.8 us (93%)
  local copies, waits for them, and re-layouts  1.56 us (5%)
  between operations  0.64 us (2%)
    pallas_call x1, Pallas kernels, on_device(): pl.pallas_call(kernel, out_shape=(pltpu.VMEM(adjoint.shape, f32), pltpu.V...  31.8 us
    unnamed x2, local copies, waits for them, and re-layouts  1.56 us

profile of v4, /device:TPU:1, one launch (start us, length us, event | category | flops | bytes accessed | tf_op | source)
XLA Modules:
  0.0 34.0 jit_solution(17862386703417173341)
XLA Ops:
  0.6 31.8 %lubrication_adjoint.1 = (f32[4,2,32,8,128]{4,3,2,1,0:T(8,128)S(1)}, f32[8,128]{1,0:T(8,128)S(1)}) custom-call(f32[4,2,32,8,128]{4,3,2,1,0:T(8,128)} %adjoint.1, f32[4,2,32,8,128]{4,3,2,1,0:T(8,128)} %source.1, f32[2,8,128]{2,1,0:T(8,128)} %pressure_in.1, f32[8,128]{1,0:T(8,128)} %film_in.1, s32[2,8,128]{2,1,0:T(8,128)} %cavity_in.1, s32[2]{0:T(128)} %temp_in.1), custom_call_target="tpu_custom_call" | custom-call | tf_op jit(solution)/shard_map/lubrication_adjoint/pallas_call | solution.py:543
  32.5 1.0 %copy.10 = f32[4,2,32,8,128]{4,3,2,1,0:T(8,128)} copy(f32[4,2,32,8,128]{4,3,2,1,0:T(8,128)S(1)} %get-tuple-element.2) | data formatting | bytes 2097152
  33.4 0.6 %copy.11 = f32[8,128]{1,0:T(8,128)} copy(f32[8,128]{1,0:T(8,128)S(1)} %get-tuple-element.3) | data formatting | bytes 8192

commit v5 on v4

--- a/solution.py
+++ b/solution.py
@@ -35,9 +35,9 @@
 def kernel(
     adjoint, source, pressure_in, film_in, cavity_in, temp_in, out, wall,
     pressure, film, cavity, temp,
-    s0, s1, halo, src, coef, pcoef, ysend, yleft, yright, mean, curv, mine, plane, mine2, ring,
+    s0, s1, halo, src, coef, pcoef, ysend, yleft, yright, mean, curv, zsum, zdiag, part, beside, mine, plane, mine2, ring,
     small_sem, in_sem, out_sem, xsend_sem, xrecv_sem, ysend_sem, yrecv_sem,
-    msend_sem, mrecv_sem, rsend_sem, rrecv_sem,
+    msend_sem, mrecv_sem, dsend_sem, drecv_sem, rsend_sem, rrecv_sem,
 ):
     nr, nt = lax.axis_size("roll"), lax.axis_size("trans")
     r, t = lax.axis_index("roll"), lax.axis_index("trans")
@@ -68,7 +68,8 @@
         pl.semaphore_signal(barrier, inc=1, device_id=plane_peer(o), device_id_type=MESH)
     for o in range(1, ZRING):
         pl.semaphore_signal(barrier, inc=1, device_id=ring_peer(o), device_id_type=MESH)
-    for peer in (up, down):
+    corners = [[(row[0], column[1]) for column in (right, left)] for row in (down, up)]
+    for peer in [up, down] + corners[0] + corners[1]:
         pl.semaphore_signal(barrier, inc=1, device_id=peer, device_id_type=MESH)
 
     smalls = [
@@ -131,10 +132,12 @@
     @pl.when(jnp.logical_not(has_left))
     def _():
         yleft[...] = jnp.zeros(yleft.shape, jnp.float32)
+        zdiag[:, 0] = jnp.zeros((2, 2, 8, NY), jnp.float32)
 
     @pl.when(jnp.logical_not(has_right))
     def _():
         yright[...] = jnp.zeros(yright.shape, jnp.float32)
+        zdiag[:, 1] = jnp.zeros((2, 2, 8, NY), jnp.float32)
 
     for copy in smalls:
         copy.wait()
@@ -170,6 +173,16 @@
             else:
                 pcoef[case, 3] = (SOUND / 12.0) * spread
 
+    for side in range(2):
+        for k in range(4):
+            zsum[side, k] = zero8
+            part[side, k] = zero8
+        for case in range(CASES):
+            for i in range(2):
+                x = (i, NX - 1 - i)[side]
+                for j, k in enumerate((A0, SLOPE, COUPLE)):
+                    part[side, 1 + j, 2 * case + i:2 * case + i + 1, :] = coef[case, k, x:x + 1, :]
+
     def x_copy(sec, grp, case, way):
         buf = (s0, s1)[sec]
         c, n = XGROUPS[sec][grp]
@@ -229,12 +242,14 @@
     def packed(acc, tile, q):
         return jnp.where(lane4 == q, pltpu.roll(tile, 4 * q + 2, 1), acc)
 
-    def inner(sec, case, comps):
+    def inner(sec, case, comps, part_of=None):
         cur, new_buf = ((s0, s1), (s1, s0))[sec]
         need_x = sorted(set(comps) | ({1} if 0 in comps else set()) | ({0} if 1 in comps else set()))
         need_y = sorted(set(comps) | ({2} if 0 in comps else set()) | ({0} if 2 in comps else set()))
 
-        def body(x, _):
+        def body(i, _):
+            x = i + 4 * (i // 2) if part_of == 0 else i
+
             def row(k):
                 return row_of(case, k, x)
 
@@ -282,7 +297,8 @@
                 ysend[1, c, case] = value
             return 0
 
-        lax.fori_loop(0, NX, body, 0, unroll=2)
+        first, last = {None: (0, NX), 0: (0, 4), 1: (2, NX - 2)}[part_of]
+        lax.fori_loop(first, last, body, 0, unroll=2)
 
     def rims(sec, case, comps):
         near, far, cross = {}, {}, {}
@@ -373,13 +389,15 @@
         accs = lax.fori_loop(0, NX, pack_rows, (zero8,) * NC)
         for c in range(NC):
             ysend[0, c, case] = accs[c]
-    pl.semaphore_wait(barrier, plane_n - 1 + ZRING - 1 + 2)
+    pl.semaphore_wait(barrier, plane_n - 1 + ZRING - 1 + 6)
     for case in range(CASES):
         x_start(0, 0, case)
         y_start(0, 0, case)
     pltpu.make_async_copy(source, source, in_sem.at[1]).wait()
     for case in range(CASES):
         inner(0, case, (0, 1, 2))
+    for case in range(CASES):
+        inner(0, case, (3,))
     for case in range(CASES):
         y_wait(0, 0, case)
         edges(0, (0,), case, (0, 1, 2))
@@ -390,63 +408,89 @@
         x_start(0, 1, case)
         x_start(1, 1, case)
 
+    def z_sum(buf, c, case, x, weights=None):
+        total = None
+        for zt in range(ZT):
+            tile = buf[c, case, x + 2, Z0 + 8 * zt:Z0 + 8 * zt + 8, :]
+            tile = tile if weights is None else tile * weights[zt]
+            total = tile if total is None else total + tile
+        return jnp.sum(total, axis=0, keepdims=True)
+
+    for side in range(2):
+        for case in range(CASES):
+            for i in range(2):
+                x = (i, NX - 1 - i)[side]
+                at = slice(2 * case + i, 2 * case + i + 1)
+                zsum[side, 0, at, :] = z_sum(s1, 0, case, x)
+                zsum[side, 1, at, :] = z_sum(s1, 2, case, x)
+                zsum[side, 2, at, :] = z_sum(s1, 1, case, x)
+                zsum[side, 3, at, :] = z_sum(s1, 0, case, x, heights)
+
+    has_row, has_column = (has_down, has_up), (has_right, has_left)
+
+    def corner_copy(side, column):
+        return pltpu.make_async_remote_copy(
+            src_ref=zsum.at[side, pl.ds(0, 2)], dst_ref=zdiag.at[1 - side, column],
+            send_sem=dsend_sem.at[side, column], recv_sem=drecv_sem.at[1 - side, column],
+            device_id=corners[side][column], device_id_type=MESH)
+
+    def corner_arrives(side, column):
+        return pltpu.make_async_remote_copy(
+            src_ref=zsum.at[side, pl.ds(0, 2)], dst_ref=zdiag.at[side, column],
+            send_sem=dsend_sem.at[side, column], recv_sem=drecv_sem.at[side, column],
+            device_id=corners[side][column], device_id_type=MESH)
+
+    def part_copy(side, slot):
+        return pltpu.make_async_remote_copy(
+            src_ref=part.at[side], dst_ref=beside.at[slot],
+            send_sem=msend_sem.at[side], recv_sem=mrecv_sem.at[slot],
+            device_id=(down, up)[side], device_id_type=MESH)
+
+    for side in range(2):
+        for column in range(2):
+            @pl.when(jnp.logical_and(has_row[side], has_column[column]))
+            def _(side=side, column=column):
+                corner_copy(side, column).start()
+
     for case in range(CASES):
         middle(0, case, (0, 1, 2))
     x_sent(0, 0)
     for case in range(CASES):
-        inner(0, case, (3,))
-    for case in range(CASES):
-        inner(1, case, (0, 1))
-
-    def mean_row(case, x):
-        total = s0[0, case, x + 2, Z0:Z0 + 8, :]
-        for zt in range(1, ZT):
-            total = total + s0[0, case, x + 2, Z0 + 8 * zt:Z0 + 8 * zt + 8, :]
-        mean[x + 2, case:case + 1, :] = jnp.sum(total, axis=0, keepdims=True)
+        inner(1, case, (0, 1), 0)
+
+    def beyond(ghost):
+        p1, m1 = pltpu.roll(ghost, NY - 1, 1), pltpu.roll(ghost, 1, 1)
+        p2, m2 = pltpu.roll(ghost, NY - 2, 1), pltpu.roll(ghost, 2, 1)
+        at0, at_end = lane == 0, lane == NY - 1
+        lo, hi = lane < 2, lane >= NY - 2
+        near = jnp.where(at_end, p1, jnp.where(at0, m1, 0.0))
+        far = jnp.where(hi, p2, jnp.where(lo, m2, 0.0))
+        near_x = jnp.where(at_end, p1, jnp.where(at0, -m1, 0.0))
+        far_x = jnp.where(hi, p2, jnp.where(lo, -m2, 0.0))
+        return 16.0 * near - far, 8.0 * near_x - far_x
+
+    for side in range(2):
+        for case in range(CASES):
+            for i in range(2):
+                x = (i, NX - 1 - i)[side]
+                part[side, 0, 2 * case + i:2 * case + i + 1, :] = z_sum(s0, 0, case, x)
+        ring_y, _unused = beyond(zsum[side, 0])
+        _unused, ring_x = beyond(zsum[side, 1])
+        part[side, 0] = part[side, 0] - part[side, 1] * ring_y - part[side, 3] * ring_x
+
+        @pl.when(has_row[side])
+        def _(side=side):
+            part_copy(side, 1 - side).start()
+    for case in range(CASES):
+        inner(1, case, (0, 1), 1)
 
     for case in range(CASES):
         y_wait(1, 0, case)
-        edges(1, (0,), case, (0,))
-        for x in (0, 1, NX - 2, NX - 1):
-            mean_row(case, x)
-
-    def m_copy(way):
-        a, b, peer = ((NX, 0, up), (2, NX + 2, down))[way]
-        return pltpu.make_async_remote_copy(
-            src_ref=mean.at[pl.ds(a, 2)], dst_ref=mean.at[pl.ds(b, 2)],
-            send_sem=msend_sem.at[way], recv_sem=mrecv_sem.at[way],
-            device_id=peer, device_id_type=MESH)
-
-    for way, ok in ((0, has_up), (1, has_down)):
-        @pl.when(ok)
-        def _(way=way):
-            m_copy(way).start()
-
-    for case in range(CASES):
-        y_wait(0, 1, case)
-        edges(0, (1,), case, (3,))
-        y_start(1, 1, case)
-        x_start(1, 2, case)
-
-    def store_out(c):
-        return [
-            pltpu.make_async_copy(
-                s0.at[c, :, 2 + x, pl.ds(Z0, NZ), :], out.at[c, :, :, x, :], out_sem.at[c])
-            for x in range(NX)
-        ]
-
-    for case in range(CASES):
-        middle(1, case, (0,))
-
-        def means(x, _, case=case):
-            mean_row(case, x)
-            return 0
-
-        lax.fori_loop(2, NX - 2, means, 0)
-        edges(1, (), case, (1,))
-        middle(1, case, (1,))
-
-        def bends(x, _, case=case):
+        edges(1, (0,), case, (0, 1))
+        middle(1, case, (0, 1))
+
+        def rows_of(x, _, case=case):
+            mean[x + 2, case:case + 1, :] = z_sum(s0, 0, case, x)
             bend = None
             for zt in range(ZT):
                 zs = Z0 + 8 * zt
@@ -456,11 +500,45 @@
             curv[case, pl.ds(x, 1), :] = jnp.sum(bend, axis=0, keepdims=True)
             return 0
 
-        lax.fori_loop(0, NX, bends, 0)
-    for way, ok in ((0, has_down), (1, has_up)):
-        @pl.when(ok)
-        def _(way=way):
-            m_copy(way).wait_recv()
+        lax.fori_loop(0, NX, rows_of, 0, unroll=2)
+
+    is_outer = sub % 2 == 0
+    for slot in range(2):
+        for column in range(2):
+            @pl.when(jnp.logical_and(has_row[slot], (has_left, has_right)[column]))
+            def _(slot=slot, column=column):
+                corner_arrives(slot, column).wait_recv()
+
+        @pl.when(has_row[slot])
+        def _(slot=slot):
+            part_copy(slot, slot).wait_recv()
+
+            def lap(v, a):
+                after, before = pltpu.roll(v, 7, 0), pltpu.roll(v, 1, 0)
+                return jnp.where(is_outer, a * v - after, -before)
+
+            sign = (1.0, -1.0)[slot]
+            a0, slope, couple = beside[slot, 1], beside[slot, 2], beside[slot, 3]
+
+            def ghost(k):
+                return jnp.where(lane >= NY - 2, zdiag[slot, 0, k], jnp.where(lane < 2, zdiag[slot, 1, k], 0.0))
+
+            lap_y, _unused = beyond(ghost(0))
+            _unused, grad_y = beyond(ghost(1))
+            value = beside[slot, 0] + a0 * (lap(zsum[slot, 0], 16.0) + lap_y)
+            value = value + sign * (slope * lap(zsum[slot, 3], 8.0) + couple * lap(zsum[slot, 2], 8.0))
+            value = value + couple * grad_y
+            for case in range(CASES):
+                for i in range(2):
+                    row = (1 - i, NX + 2 + i)[slot]
+                    mean[row, case:case + 1, :] = value[2 * case + i:2 * case + i + 1, :]
+
+    def store_out(c):
+        return [
+            pltpu.make_async_copy(
+                s0.at[c, :, 2 + x, pl.ds(Z0, NZ), :], out.at[c, :, :, x, :], out_sem.at[c])
+            for x in range(NX)
+        ]
 
     grad = jnp.zeros((NX, NY), jnp.float32)
     for case in range(CASES):
@@ -494,6 +572,11 @@
     for o in sorted(range(1, plane_n), key=lambda o: -hops(o)):
         plane_copy(o).start()
 
+    for case in range(CASES):
+        y_wait(0, 1, case)
+        edges(0, (1,), case, (3,))
+        y_start(1, 1, case)
+        x_start(1, 2, case)
     for c in (0, 1):
         for copy in store_out(c):
             copy.start()
@@ -519,10 +602,14 @@
 
     pltpu.make_async_copy(plane.at[pl.ds(1, plane_n - 1)], plane.at[pl.ds(1, plane_n - 1)], rsend_sem.at[0]).wait()
     pltpu.make_async_copy(ring.at[pl.ds(1, ZRING - 1)], ring.at[pl.ds(1, ZRING - 1)], rsend_sem.at[1]).wait()
-    for way, ok in ((0, has_up), (1, has_down)):
-        @pl.when(ok)
-        def _(way=way):
-            m_copy(way).wait_send()
+    for side in range(2):
+        @pl.when(has_row[side])
+        def _(side=side):
+            part_copy(side, 1 - side).wait_send()
+        for column in range(2):
+            @pl.when(jnp.logical_and(has_row[side], has_column[column]))
+            def _(side=side, column=column):
+                corner_copy(side, column).wait_send()
     for grp in range(3):
         x_sent(1, grp)
     for sec in range(2):
@@ -561,6 +648,10 @@
             pltpu.VMEM((2, NC, CASES, 8, NY), f32),
             pltpu.VMEM((NX + 4, CASES, NY), f32),
             pltpu.VMEM((CASES, NX, NY), f32),
+            pltpu.VMEM((2, 4, 8, NY), f32),
+            pltpu.VMEM((2, 2, 2, 8, NY), f32),
+            pltpu.VMEM((2, 4, 8, NY), f32),
+            pltpu.VMEM((2, 4, 8, NY), f32),
             pltpu.VMEM((1, 1, NY), f32),
             pltpu.VMEM((32, 1, NY), f32),
             pltpu.VMEM((1, 1, NY), f32),
@@ -574,6 +665,8 @@
             dma((2, 2, CASES, 2)),
             dma((2,)),
             dma((2,)),
+            dma((2, 2)),
+            dma((2, 2)),
             dma((2,)),
             dma((2,)),
         ],

time: 34.1 us -> 33.7 us (0.988)
  Pallas kernels: 31.8 us -> 31.4 us
    pallas_call x1, Pallas kernels: 31.8 us -> 31.4 us  [on_device(): pl.pallas_call(kernel, out_shape=(pltpu.VMEM(adjoint.shape, f32), pltpu.V...]
where the time goes in v5:
time: 33.7 us; the launch traced here: 33.6 us
  Pallas kernels  31.4 us (93%)
  local copies, waits for them, and re-layouts  1.56 us (5%)
  between operations  0.64 us (2%)
    pallas_call x1, Pallas kernels, on_device(): pl.pallas_call(kernel, out_shape=(pltpu.VMEM(adjoint.shape, f32), pltpu.V...  31.4 us
    unnamed x2, local copies, waits for them, and re-layouts  1.56 us

profile of v5, /device:TPU:1, one launch (start us, length us, event | category | flops | bytes accessed | tf_op | source)
XLA Modules:
  0.0 33.6 jit_solution(1442511291688736679)
XLA Ops:
  0.6 31.4 %lubrication_adjoint.1 = (f32[4,2,32,8,128]{4,3,2,1,0:T(8,128)S(1)}, f32[8,128]{1,0:T(8,128)S(1)}) custom-call(f32[4,2,32,8,128]{4,3,2,1,0:T(8,128)} %adjoint.1, f32[4,2,32,8,128]{4,3,2,1,0:T(8,128)} %source.1, f32[2,8,128]{2,1,0:T(8,128)} %pressure_in.1, f32[8,128]{1,0:T(8,128)} %film_in.1, s32[2,8,128]{2,1,0:T(8,128)} %cavity_in.1, s32[2]{0:T(128)} %temp_in.1), custom_call_target="tpu_custom_call" | custom-call | tf_op jit(solution)/shard_map/lubrication_adjoint/pallas_call | solution.py:630
  32.0 1.0 %copy.10 = f32[4,2,32,8,128]{4,3,2,1,0:T(8,128)} copy(f32[4,2,32,8,128]{4,3,2,1,0:T(8,128)S(1)} %get-tuple-element.2) | data formatting | bytes 2097152
  33.0 0.6 %copy.11 = f32[8,128]{1,0:T(8,128)} copy(f32[8,128]{1,0:T(8,128)S(1)} %get-tuple-element.3) | data formatting | bytes 8192

commit v6 on v5

--- a/solution.py
+++ b/solution.py
@@ -37,7 +37,7 @@
     pressure, film, cavity, temp,
     s0, s1, halo, src, coef, pcoef, ysend, yleft, yright, mean, curv, zsum, zdiag, part, beside, mine, plane, mine2, ring,
     small_sem, in_sem, out_sem, xsend_sem, xrecv_sem, ysend_sem, yrecv_sem,
-    msend_sem, mrecv_sem, dsend_sem, drecv_sem, rsend_sem, rrecv_sem,
+    msend_sem, mrecv_sem, dsend_sem, drecv_sem, rsend_sem, rrecv_sem, word,
 ):
     nr, nt = lax.axis_size("roll"), lax.axis_size("trans")
     r, t = lax.axis_index("roll"), lax.axis_index("trans")
@@ -64,12 +64,27 @@
     has_right, has_left = t < nt - 1, t > 0
 
     barrier = pltpu.get_barrier_semaphore()
-    for o in range(1, plane_n):
-        pl.semaphore_signal(barrier, inc=1, device_id=plane_peer(o), device_id_type=MESH)
-    for o in range(1, ZRING):
-        pl.semaphore_signal(barrier, inc=1, device_id=ring_peer(o), device_id_type=MESH)
+    def hops(o):
+        dt = o // (2 * groups)
+        return min(dt % 4, 4 - dt % 4) + 2 * (dt >= 4) + (o // 2) % groups
+
+    far_plane = sorted(range(1, plane_n), key=lambda o: -hops(o))
+    far_ring = sorted(range(1, ZRING), key=lambda o: -min(o, ZRING - o))
     corners = [[(row[0], column[1]) for column in (right, left)] for row in (down, up)]
-    for peer in [up, down] + corners[0] + corners[1]:
+    y_phys = 2 * (t // 4) + g
+
+    def in_plane(dx, dy, dc):
+        y = lax.rem(y_phys + dy + 4, 4)
+        row = ((lax.rem(y, 2)) * ZRING + z) * 2 + lax.rem(core + dc, 2)
+        return (row, (y // 2) * 4 + lax.rem(lax.rem(t, 4) + dx + 4, 4))
+
+    close = [
+        in_plane(dx, dy, dc)
+        for dx in (2, 1, -1, 0) for dy in (2, 1, -1, 0) for dc in (1, 0)
+        if (dx, dy, dc) != (0, 0, 0) and abs(dx) + abs(dy) <= 2
+    ]
+    partners = [right, left, up, down] + [ring_peer(o) for o in (2, ZRING - 2, 1, ZRING - 1)] + close
+    for peer in partners:
         pl.semaphore_signal(barrier, inc=1, device_id=peer, device_id_type=MESH)
 
     smalls = [
@@ -389,10 +404,13 @@
         accs = lax.fori_loop(0, NX, pack_rows, (zero8,) * NC)
         for c in range(NC):
             ysend[0, c, case] = accs[c]
-    pl.semaphore_wait(barrier, plane_n - 1 + ZRING - 1 + 6)
+    pl.semaphore_wait(barrier, len(partners))
+    for case in range(CASES):
+        y_start(0, 0, case)
     for case in range(CASES):
         x_start(0, 0, case)
-        y_start(0, 0, case)
+    for peer in partners:
+        pl.semaphore_signal(word, inc=1, device_id=peer, device_id_type=MESH)
     pltpu.make_async_copy(source, source, in_sem.at[1]).wait()
     for case in range(CASES):
         inner(0, case, (0, 1, 2))
@@ -407,6 +425,8 @@
         y_start(0, 1, case)
         x_start(0, 1, case)
         x_start(1, 1, case)
+
+    pl.semaphore_wait(word, len(partners))
 
     def z_sum(buf, c, case, x, weights=None):
         total = None
@@ -565,11 +585,7 @@
             src_ref=mine2.at[0], dst_ref=ring.at[o], send_sem=rsend_sem.at[1], recv_sem=rrecv_sem.at[1],
             device_id=ring_peer(o), device_id_type=MESH)
 
-    def hops(o):
-        dt = o // (2 * groups)
-        return min(dt % 4, 4 - dt % 4) + 2 * (dt >= 4) + (o // 2) % groups
-
-    for o in sorted(range(1, plane_n), key=lambda o: -hops(o)):
+    for o in far_plane:
         plane_copy(o).start()
 
     for case in range(CASES):
@@ -587,7 +603,7 @@
         inner(1, case, (2, 3))
     pltpu.make_async_copy(plane.at[pl.ds(1, plane_n - 1)], plane.at[pl.ds(1, plane_n - 1)], rrecv_sem.at[0]).wait()
     mine2[0] = mine[0] + jnp.sum(plane[1:plane_n], axis=0)
-    for o in sorted(range(1, ZRING), key=lambda o: -min(o, ZRING - o)):
+    for o in far_ring:
         ring_copy(o).start()
     for case in range(CASES):
         y_wait(1, 1, case)
@@ -596,10 +612,6 @@
     for c in (2, 3):
         for copy in store_out(c):
             copy.start()
-    pltpu.make_async_copy(ring.at[pl.ds(1, ZRING - 1)], ring.at[pl.ds(1, ZRING - 1)], rrecv_sem.at[1]).wait()
-    total = jnp.sum(mine2[0] + jnp.sum(ring[1:ZRING], axis=0), axis=1, keepdims=True)
-    wall[...] = wall[...] / jnp.sqrt(total / cells + 1e-06)
-
     pltpu.make_async_copy(plane.at[pl.ds(1, plane_n - 1)], plane.at[pl.ds(1, plane_n - 1)], rsend_sem.at[0]).wait()
     pltpu.make_async_copy(ring.at[pl.ds(1, ZRING - 1)], ring.at[pl.ds(1, ZRING - 1)], rsend_sem.at[1]).wait()
     for side in range(2):
@@ -616,6 +628,10 @@
         y_sent(sec)
     for c in range(NC):
         pltpu.make_async_copy(out.at[c], out.at[c], out_sem.at[c]).wait()
+
+    pltpu.make_async_copy(ring.at[pl.ds(1, ZRING - 1)], ring.at[pl.ds(1, ZRING - 1)], rrecv_sem.at[1]).wait()
+    total = jnp.sum(mine2[0] + jnp.sum(ring[1:ZRING], axis=0), axis=1, keepdims=True)
+    wall[...] = wall[...] / jnp.sqrt(total / cells + 1e-06)
 
 
 def on_device(adjoint, source, pressure, film, cavity, temp_index):
@@ -669,6 +685,7 @@
             dma((2, 2)),
             dma((2,)),
             dma((2,)),
+            pltpu.SemaphoreType.REGULAR,
         ],
         compiler_params=pltpu.CompilerParams(
             collective_id=0, has_side_effects=True, vmem_limit_bytes=48 * 1024 * 1024

time: 33.7 us -> 33.1 us (0.982)
  Pallas kernels: 31.4 us -> 30.8 us
    pallas_call x1, Pallas kernels: 31.4 us -> 30.8 us  [on_device(): pl.pallas_call(kernel, out_shape=(pltpu.VMEM(adjoint.shape, f32), pltpu.V...]
where the time goes in v6:
time: 33.1 us; the launch traced here: 33 us
  Pallas kernels  30.8 us (93%)
  local copies, waits for them, and re-layouts  1.56 us (5%)
  between operations  0.64 us (2%)
    pallas_call x1, Pallas kernels, on_device(): pl.pallas_call(kernel, out_shape=(pltpu.VMEM(adjoint.shape, f32), pltpu.V...  30.8 us
    unnamed x2, local copies, waits for them, and re-layouts  1.56 us

profile of v6, /device:TPU:1, one launch (start us, length us, event | category | flops | bytes accessed | tf_op | source)
XLA Modules:
  0.0 33.0 jit_solution(7139000447621410849)
XLA Ops:
  0.6 30.8 %lubrication_adjoint.1 = (f32[4,2,32,8,128]{4,3,2,1,0:T(8,128)S(1)}, f32[8,128]{1,0:T(8,128)S(1)}) custom-call(f32[4,2,32,8,128]{4,3,2,1,0:T(8,128)} %adjoint.1, f32[4,2,32,8,128]{4,3,2,1,0:T(8,128)} %source.1, f32[2,8,128]{2,1,0:T(8,128)} %pressure_in.1, f32[8,128]{1,0:T(8,128)} %film_in.1, s32[2,8,128]{2,1,0:T(8,128)} %cavity_in.1, s32[2]{0:T(128)} %temp_in.1), custom_call_target="tpu_custom_call" | custom-call | tf_op jit(solution)/shard_map/lubrication_adjoint/pallas_call | solution.py:646
  31.4 1.0 %copy.10 = f32[4,2,32,8,128]{4,3,2,1,0:T(8,128)} copy(f32[4,2,32,8,128]{4,3,2,1,0:T(8,128)S(1)} %get-tuple-element.2) | data formatting | bytes 2097152
  32.4 0.6 %copy.11 = f32[8,128]{1,0:T(8,128)} copy(f32[8,128]{1,0:T(8,128)S(1)} %get-tuple-element.3) | data formatting | bytes 8192

commit v7 on v6

--- a/solution.py
+++ b/solution.py
@@ -22,6 +22,7 @@
 Z0 = 8
 ZROWS = 48
 ZT = NZ // 8
+PIECES = 4
 ZRING = 8
 XGROUPS = (((0, 3), (3, 1)), ((0, 2), (2, 1), (3, 1)))
 YGROUPS = (((0, 3), (3, 1)), ((0, 3), (3, 1)))
@@ -393,17 +394,21 @@
         lax.fori_loop(2, NX - 2, body, 0)
 
     pltpu.make_async_copy(adjoint, adjoint, in_sem.at[0]).wait()
-    for case in range(CASES):
-        def pack_rows(x, accs, case=case):
+    def pack_state(case, first, last):
+        def pack_rows(x, accs):
             accs = list(accs)
-            for c in range(NC):
+            for c in range(first, last):
                 for zt in range(ZT):
-                    accs[c] = packed(accs[c], s0[c, case, x + 2, Z0 + 8 * zt:Z0 + 8 * zt + 8, :], x * ZT + zt)
+                    tile = s0[c, case, x + 2, Z0 + 8 * zt:Z0 + 8 * zt + 8, :]
+                    accs[c - first] = packed(accs[c - first], tile, x * ZT + zt)
             return tuple(accs)
 
-        accs = lax.fori_loop(0, NX, pack_rows, (zero8,) * NC)
-        for c in range(NC):
-            ysend[0, c, case] = accs[c]
+        accs = lax.fori_loop(0, NX, pack_rows, (zero8,) * (last - first), unroll=2)
+        for c in range(first, last):
+            ysend[0, c, case] = accs[c - first]
+
+    for case in range(CASES):
+        pack_state(case, 0, 3)
     pl.semaphore_wait(barrier, len(partners))
     for case in range(CASES):
         y_start(0, 0, case)
@@ -415,6 +420,7 @@
     for case in range(CASES):
         inner(0, case, (0, 1, 2))
     for case in range(CASES):
+        pack_state(case, 3, 4)
         inner(0, case, (3,))
     for case in range(CASES):
         y_wait(0, 0, case)
@@ -634,6 +640,18 @@
     wall[...] = wall[...] / jnp.sqrt(total / cells + 1e-06)
 
 
+def store(state, wall, state_out, wall_out, sem):
+    n = NC // PIECES
+    copies = [pltpu.make_async_copy(wall, wall_out, sem.at[PIECES])] + [
+        pltpu.make_async_copy(state.at[pl.ds(n * k, n)], state_out.at[pl.ds(n * k, n)], sem.at[k])
+        for k in range(PIECES)
+    ]
+    for copy in copies:
+        copy.start()
+    for copy in copies:
+        copy.wait()
+
+
 def on_device(adjoint, source, pressure, film, cavity, temp_index):
     vmem = pl.BlockSpec(memory_space=pltpu.VMEM)
     hbm = pl.BlockSpec(memory_space=pltpu.HBM)
@@ -643,7 +661,7 @@
         pltpu.with_memory_space_constraint(a, pltpu.HBM)
         for a in (adjoint, source, pressure, film, cavity, temp_index)
     ]
-    return pl.pallas_call(
+    state, wall = pl.pallas_call(
         kernel,
         out_shape=(pltpu.VMEM(adjoint.shape, f32), pltpu.VMEM(film.shape, f32)),
         in_specs=[hbm] * 6,
@@ -692,6 +710,14 @@
         ),
         name="lubrication_adjoint",
     )(*given)
+    return pl.pallas_call(
+        store,
+        out_shape=(pltpu.HBM(adjoint.shape, f32), pltpu.HBM(film.shape, f32)),
+        in_specs=[vmem, vmem],
+        out_specs=(hbm, hbm),
+        scratch_shapes=[dma((PIECES + 1,))],
+        name="store",
+    )(*[pltpu.with_memory_space_constraint(a, pltpu.VMEM) for a in (state, wall)])
 
 
 def solution(mesh):

time: 33.1 us -> 32.2 us (0.973)
  local copies, waits for them, and re-layouts: 1.56 us -> 0 us
  Pallas kernels: 30.8 us -> 31.5 us
    unnamed x2 -> x0, local copies, waits for them, and re-layouts: 1.56 us -> none
    pallas_call x0 -> x1, Pallas kernels: none -> 1.01 us  [on_device(): pl.pallas_call(store, out_shape=(pltpu.HBM(adjoint.shape, f32), pltpu.HBM...]
where the time goes in v7:
time: 32.2 us; the launch traced here: 32.1 us
  Pallas kernels  31.5 us (98%)
  between operations  0.64 us (2%)
    pallas_call x1, Pallas kernels, on_device(): pl.pallas_call(kernel, out_shape=(pltpu.VMEM(adjoint.shape, f32), pltpu.V...  30.4 us
    pallas_call x1, Pallas kernels, on_device(): pl.pallas_call(store, out_shape=(pltpu.HBM(adjoint.shape, f32), pltpu.HBM...  1.01 us

profile of v7, /device:TPU:1, one launch (start us, length us, event | category | flops | bytes accessed | tf_op | source)
XLA Modules:
  0.0 32.1 jit_solution(16751650974615878247)
XLA Ops:
  0.6 30.4 %lubrication_adjoint.1 = (f32[4,2,32,8,128]{4,3,2,1,0:T(8,128)S(1)}, f32[8,128]{1,0:T(8,128)S(1)}) custom-call(f32[4,2,32,8,128]{4,3,2,1,0:T(8,128)} %adjoint.1, f32[4,2,32,8,128]{4,3,2,1,0:T(8,128)} %source.1, f32[2,8,128]{2,1,0:T(8,128)} %pressure_in.1, f32[8,128]{1,0:T(8,128)} %film_in.1, s32[2,8,128]{2,1,0:T(8,128)} %cavity_in.1, s32[2]{0:T(128)} %temp_in.1), custom_call_target="tpu_custom_call" | custom-call | tf_op jit(solution)/shard_map/lubrication_adjoint/pallas_call | solution.py:664
  31.1 1.0 %store.1 = (f32[4,2,32,8,128]{4,3,2,1,0:T(8,128)}, f32[8,128]{1,0:T(8,128)}) custom-call(f32[4,2,32,8,128]{4,3,2,1,0:T(8,128)S(1)} %get-tuple-element.4.state, f32[8,128]{1,0:T(8,128)S(1)} %get-tuple-element.5.wall), custom_call_target="tpu_custom_call" | custom-call | tf_op jit(solution)/shard_map/store/pallas_call | solution.py:713
